TPU v7x, 32 devices: a whole 2x2x4 slice. The times are simulated.
32 devices in a mesh: group: 4 (over y, x), shard: 8 (over z, core).
Axes of the slice: x: 2, y: 2, z: 4, core: 2. Of those that a mesh axis runs over, the one named last changes fastest.
Arguments:
- tokens: bfloat16 [32, 192, 768], P(('group', 'shard')), may hold values from -650 to 650
- norm_gain: float32 [768], replicated, may hold values from 0.1 to 1.9
- w_query: bfloat16 [768, 768], P('shard'), may hold values from -8 to 8
- w_key: bfloat16 [768, 768], P('shard'), may hold values from -0.21875 to 0.21875
- w_value: bfloat16 [768, 768], P('shard'), may hold values from -0.625 to 0.625
- w_out: bfloat16 [768, 768], P('shard'), may hold values from -0.21875 to 0.21875
- owner_map: int32 [4, 8], P('group'), may hold values from 0 to 7, each once within a row
- pair_images: int32 [256, 2], P(('group', 'shard')), may hold values from 0 to 7, as said below
- pair_count: int32 [32], P(('group', 'shard')), may hold values from 1 to 8, 128 in all
- confidence: int32 [256, 2], P(('group', 'shard')), may hold values from 1 to 8
Outputs:
- updated: bfloat16 [32, 192, 768], P(('group', 'shard'))
Inputs may be any that keep to these rules, and one draw needn't show every extreme that they name: `pair_images`: each row names two different images of the listing device's own group, by their index within that group. Device d lists its pairs in its first pair_count[d] rows of pair_images and confidence; the other rows are unused.
All inputs are finite; a program needn't handle non-finite values.
Results may differ from a plain program's by a relative error of at most 0.013.
The roundings to bfloat16 on the way count: a program that leaves them out, or rounds other values in their place, can miss the bound.
Values may be sent and summed in bfloat16 or wider, within the bound.
No kernel may reach another device: no remote copies, remote signals or barrier semaphores. Data moves between devices by JAX's collectives and lax.ppermute only.
A program may use at most 128 MiB of HBM per device.

v0:
```python
import functools
import math

import jax
import jax.numpy as jnp
from jax import lax
from jax.experimental import pallas as pl
from jax.experimental.pallas import tpu as pltpu
from jax.sharding import PartitionSpec as P


HEADS = 12
HEAD_DIM = 64
TOGETHER = 4

F32 = jnp.float32
BF16 = jnp.bfloat16
HBM_SPEC = pl.BlockSpec(memory_space=pltpu.HBM)
SMEM_SPEC = pl.BlockSpec(memory_space=pltpu.SMEM)
VMEM_SPEC = pl.BlockSpec(memory_space=pltpu.VMEM)


def round_up(value, multiple):
    return -(-value // multiple) * multiple


def struct(shape, dtype=BF16):
    return jax.ShapeDtypeStruct(shape, dtype)


def call(kernel, out_shape, smem, vmem, scratch=(), megabytes=16, whole=()):
    many = isinstance(out_shape, (tuple, list))
    return pl.pallas_call(
        kernel,
        out_shape=tuple(out_shape) if many else out_shape,
        in_specs=[SMEM_SPEC] * len(smem) + [VMEM_SPEC] * len(vmem) + [HBM_SPEC] * len(whole),
        out_specs=(VMEM_SPEC,) * len(out_shape) if many else VMEM_SPEC,
        scratch_shapes=list(scratch),
        compiler_params=pltpu.CompilerParams(vmem_limit_bytes=megabytes * 1024 * 1024),
    )(*smem, *vmem, *whole)


def places(members):
    position = lax.axis_index("shard")
    return position // members, position % members


def direction_table(owner_ref, pairs_ref, count_ref, conf_ref, shape):
    row = lax.broadcasted_iota(jnp.int32, shape, 0)
    column = lax.broadcasted_iota(jnp.int32, shape, 1)
    table = jnp.zeros(shape, jnp.int32)
    for p in range(pairs_ref.shape[1]):
        first = owner_ref[0, pairs_ref[0, p]]
        second = owner_ref[0, pairs_ref[1, p]]
        listed = p < count_ref[0]
        forward = jnp.where(listed, conf_ref[0, p], 0)
        backward = jnp.where(listed, conf_ref[1, p], 0)
        table += jnp.where((row == first) & (column == second), forward, 0)
        table += jnp.where((row == second) & (column == first), backward, 0)
    return table.astype(F32)


def table_kernel(owner_ref, pairs_ref, count_ref, conf_ref, table_ref):
    table_ref[...] = direction_table(owner_ref, pairs_ref, count_ref, conf_ref, table_ref.shape).astype(BF16)


def message_kernel(cfg, *refs):
    groups, members, sharers = cfg
    sources, refs = refs[:10], refs[10:]
    normed_ref, own_ref, message_refs, refs = refs[0], refs[1], refs[2 : 1 + groups], refs[1 + groups :]
    copied, wide, sem = refs[:10], refs[10], refs[11]
    owner_ref, pairs_ref, count_ref, conf_ref, query_ref, key_ref, value_ref, out_ref, tokens_ref, gain_ref = copied
    copies = [pltpu.make_async_copy(source, into, sem.at[i]) for i, (source, into) in enumerate(zip(sources, copied))]
    for each in copies:
        each.start()
    own, _ = places(members)
    rows, features = query_ref.shape
    width = features // groups
    part = rows // sharers
    start = pl.multiple_of(lax.axis_index("group") * part, 8)
    lanes = own_ref.shape[1]
    for each in copies:
        each.wait()
    for i, ref in enumerate((key_ref, value_ref, query_ref, out_ref)):
        wide[i] = ref[...].astype(F32)
    for h in range(groups):
        cut = slice(h * width, (h + 1) * width)

        @pl.when(own == h)
        def _(cut=cut):
            for i, ref in enumerate((key_ref, value_ref, query_ref)):
                own_ref[:, i * width : (i + 1) * width] = ref[:, cut]

        for k in range(1, groups):

            @pl.when(own == h ^ k)
            def _(k=k, cut=cut):
                for i in range(3):
                    message_refs[k - 1][:, i * width : (i + 1) * width] = wide[i, pl.ds(start, part), cut].astype(BF16)

    images = groups * members
    table = direction_table(owner_ref, pairs_ref, count_ref, conf_ref, (images, lanes - 3 * width)).astype(BF16)
    own_ref[:images, 3 * width :] = table
    for ref in message_refs:
        ref[:, lanes:] = wide[3, pl.ds(start, part), :].astype(BF16)
        ref[:images, 3 * width : lanes] = table
    normed_ref[...] = layer_norm(tokens_ref[...], gain_ref[...])


def layer_norm(tokens, gain):
    values = tokens.astype(F32)
    average = jnp.mean(values, axis=-1, keepdims=True)
    centred = values - average
    variance = jnp.mean(centred * centred, axis=-1, keepdims=True)
    return (centred * lax.rsqrt(variance + 1e-05) * gain.reshape(1, gain.shape[0])).astype(BF16)


def norm_kernel(tokens_ref, gain_ref, normed_ref):
    normed_ref[...] = layer_norm(tokens_ref[...], gain_ref[...])


def packed_kernel(*refs):
    message_refs, packed_ref = refs[:-1], refs[-1]
    part = message_refs[0].shape[0]
    for k, ref in enumerate(message_refs):
        packed_ref[k * part : (k + 1) * part] = ref[...]


def gathered_kernel(cfg, own_ref, out_ref, *refs):
    groups, rows, sharers, images, spare = cfg
    shared_refs = refs[:sharers]
    in_block, out_block, wide = refs[sharers:]
    part = rows // sharers
    lanes = in_block.shape[1]
    mine = lax.axis_index("group")
    in_block[:rows] = own_ref[...]
    out_block[:rows] = out_ref[...]
    for j in range(sharers):
        for k in range(1, groups):
            start = pl.multiple_of((k - 1) * rows + jnp.bitwise_xor(mine, j) * part, 8)
            wide[pl.ds(start, part), :] = shared_refs[j][(k - 1) * part : k * part, :].astype(F32)
    in_block[rows:] = wide[:, :lanes].astype(BF16)
    out_block[rows:] = wide[:, lanes:].astype(BF16)
    for k in range(1, groups):
        in_block[k * rows : k * rows + images, spare:] = shared_refs[0][(k - 1) * part : (k - 1) * part + images, spare:lanes]


def joined_kernel(cfg, mine_ref, other_ref, whole_ref):
    groups, members, rows = cfg
    own, member = places(members)
    for k in range(groups):
        source = jnp.bitwise_xor(own, k) * members
        for ref, who in ((mine_ref, member), (other_ref, 1 - member)):
            start = pl.multiple_of((source + who) * rows, 16)
            whole_ref[pl.ds(start, rows), :] = ref[k * rows : (k + 1) * rows, :]


def attention_kernel(cfg, *refs):
    groups, members, heads, low, high, slots, last = cfg
    refs = list(refs)
    take = lambda count: [refs.pop(0) for _ in range(count)]
    table_ref, weights = take(2)
    image_refs = take(len(slots))
    first = low < 0
    state_in = [] if first else take(5)
    out_refs = take(groups) if last else []
    key_ref, value_ref, query_ref, pair_ref, single_ref = take(5)
    pictures, list_ref = take(2)
    images = groups * members
    own, member = places(members)
    width = heads * HEAD_DIM
    length = image_refs[0].shape[0]
    ahead = 2 * member - 1

    for ref, (step, flip) in zip(image_refs, slots):
        if step is None:
            pictures[flip // members, (flip % members) * length : (flip % members + 1) * length, :] = ref[...]
            continue
        place = own + step * ahead
        who = jnp.bitwise_xor(member, flip)

        @pl.when((place >= 0) & (place < groups))
        def _(ref=ref, place=place, who=who):
            pictures[place, pl.ds(pl.multiple_of(who * length, 16), length), :] = ref[...]

    if first:
        pair_ref[...] = jnp.zeros_like(pair_ref)
        single_ref[...] = jnp.zeros_like(single_ref)
    else:
        for new, old in zip((key_ref, value_ref, query_ref, pair_ref, single_ref), state_in):
            new[...] = old[...]

    count = jnp.int32(0)
    for place in range(groups):
        for target in range(images):
            away = jnp.maximum(jnp.abs(place - own), jnp.abs(target // members - own))
            amount = table_ref[place * members + member, target]
            list_ref[count] = place * images + target
            count = count + ((amount > 0) & (away > low) & (away <= high)).astype(jnp.int32)

    def project(place, carry):
        away = jnp.abs(place - own)

        @pl.when((away > low) & (away <= high))
        def _():
            both = jnp.dot(pictures[place], weights[:, : 2 * width], preferred_element_type=F32).astype(BF16)
            aligned = width // 128 * 128
            for who in range(members):
                rows = both[who * length : (who + 1) * length]
                key_ref[place * members + who] = rows[:, :width]
                value_ref[place * members + who] = rows[:, aligned:].T[width - aligned :]
            rows = pictures[place, pl.ds(pl.multiple_of(member * length, 16), length), :]
            query = jnp.dot(rows, weights[:, 2 * width : 3 * width], preferred_element_type=F32).astype(BF16)
            flipped = query.T
            head = lax.broadcasted_iota(jnp.int32, flipped.shape, 0) // HEAD_DIM
            for h in range(heads):
                query_ref[place, :, h * length : (h + 1) * length] = jnp.where(
                    head == h, flipped, jnp.zeros_like(flipped)
                )

        return carry

    lax.fori_loop(0, groups, project, 0)

    scale = math.log2(math.e) / math.sqrt(HEAD_DIM)
    paired = heads // 2

    def block(number, carry):
        entries = []
        for u in range(TOGETHER):
            at = number * TOGETHER + u
            there = at < count
            entry = list_ref[jnp.where(there, at, 0)]
            place, target = entry // images, entry % images
            amount = jnp.where(there, table_ref[place * members + member, target], 0.0)
            entries.append((place, target, amount))
        scores = [jnp.dot(key_ref[t], query_ref[s], preferred_element_type=F32) for s, t, _ in entries]
        expos, factors = [], []
        for each, (_, _, amount) in zip(scores, entries):
            largest = jnp.max(each, axis=0, keepdims=True)
            expo = jnp.exp2((each - largest) * scale)
            total = jnp.sum(expo, axis=0, keepdims=True)
            expos.append(expo.astype(BF16))
            factors.append(amount / total)
        parts = []
        for (_, target, _), expo, factor in zip(entries, expos, factors):
            for j in range(paired):
                rows, lanes = slice(2 * j * HEAD_DIM, 2 * (j + 1) * HEAD_DIM), slice(2 * j * length, 2 * (j + 1) * length)
                part = jnp.dot(value_ref[target, rows, :], expo[:, lanes], preferred_element_type=F32)
                parts.append(part * factor[:, lanes])
            if heads % 2:
                rows, lanes = slice((heads - 1) * HEAD_DIM, None), slice((heads - 1) * length, None)
                part = jnp.dot(value_ref[target, rows, :], expo[:, lanes], preferred_element_type=F32)
                parts.append(part * factor[:, lanes])
        for place, _, _ in entries:
            for j in range(paired):
                pair_ref[place, j] += parts.pop(0)
            if heads % 2:
                single_ref[place] += parts.pop(0)
        return carry

    lax.fori_loop(0, (count + TOGETHER - 1) // TOGETHER, block, 0)

    if last:
        for k in range(groups):
            place = jnp.bitwise_xor(own, k)
            total = jnp.float32(1.0)
            for target in range(images):
                total += table_ref[place * members + member, target]
            pieces = []
            for h in range(heads):
                if h == heads - 1 and heads % 2:
                    pieces.append(single_ref[place])
                else:
                    at = h % 2
                    pieces.append(
                        pair_ref[place, h // 2, at * HEAD_DIM : (at + 1) * HEAD_DIM, at * length : (at + 1) * length]
                    )
            whole = (jnp.concatenate(pieces, axis=0) / total).astype(BF16).T
            half = length // 2
            out_refs[k][:, :width] = whole[:half]
            out_refs[k][:, width:] = whole[half:]


def output_kernel(cfg, *refs):
    groups, members = cfg
    weights = refs[0]
    part_refs = refs[1 : 1 + groups]
    out_ref, gathered = refs[1 + groups :]
    own, _ = places(members)
    half = part_refs[0].shape[0]
    width = part_refs[0].shape[1] // 2
    for k in range(groups):
        source = jnp.bitwise_xor(own, k)
        gathered[source, :half] = part_refs[k][:, :width]
        gathered[source, half:] = part_refs[k][:, width:]
    whole = jnp.concatenate([gathered[h] for h in range(groups)], axis=1)
    out_ref[...] = jnp.dot(whole, weights[...], preferred_element_type=F32).astype(BF16)


def shards(mesh_shape, *arrays):
    return device_step(mesh_shape, *arrays)


def device_step(mesh_shape, tokens, norm_gain, w_query, w_key, w_value, w_out, owner_map, pair_images, pair_count, confidence):
    devices, sharers = mesh_shape["shard"], mesh_shape["group"]
    groups = math.gcd(HEADS & -HEADS, devices)
    members = devices // groups
    heads = HEADS // groups
    width = heads * HEAD_DIM
    length, features = tokens.shape[1:]
    rows = w_query.shape[0]
    small = (owner_map, pair_images.T, pair_count, confidence.T)
    lanes = round_up(3 * width + devices, 128)
    relayed = members == 2 and sharers & (sharers - 1) == 0
    relayed = relayed and rows % (8 * sharers) == 0 and rows % 16 == 0 and rows // sharers >= devices
    relayed = relayed and devices % 8 == 0 and (groups - 1) * rows % 16 == 0
    across = lambda k: [(i, i ^ (k * members)) for i in range(devices)]
    exchange = lambda x, k: lax.ppermute(x, "shard", across(k))

    stage_images, stage_slots = [], []
    if relayed:
        part = rows // sharers
        swap = lambda x: lax.ppermute(x, "shard", [(i, i ^ 1) for i in range(devices)])
        share = lambda x, j: lax.ppermute(
            x,
            ("group", "shard"),
            [(g * devices + i, (g ^ j) * devices + i) for g in range(sharers) for i in range(devices)],
        )
        arrays = (w_query, w_key, w_value, w_out, tokens[0], norm_gain)
        normed, own_block, *messages = call(
            functools.partial(message_kernel, (groups, members, sharers)),
            [struct((length, features)), struct((rows, lanes))] + [struct((part, lanes + features))] * (groups - 1),
            (),
            (),
            [pltpu.SMEM(x.shape, x.dtype) for x in small]
            + [pltpu.VMEM(x.shape, x.dtype) for x in arrays]
            + [pltpu.VMEM((4, rows, features), F32), pltpu.SemaphoreType.DMA((10,))],
            megabytes=62,
            whole=(*small, *arrays),
        )
        messages = [exchange(messages[k - 1], k) for k in range(1, groups)]
        own_a, own_b = normed, swap(normed)
        images, slots = [own_a, own_b], [(0, 0), (0, 1)]
        a, b = own_a, own_b
        for k in range(1, groups):
            pairs = [(2 * z, 2 * z + 2) for z in range(k - 1, groups - 1)]
            pairs += [(2 * z + 1, 2 * z - 1) for z in range(1, groups - k + 1)]
            a, b = lax.ppermute(a, "shard", pairs), lax.ppermute(b, "shard", pairs)
            images += [a, b, swap(a), swap(b)]
            slots += [(k, 0), (k, 1), (-k, 1), (-k, 0)]
            if k == 1 or k == groups - 1:
                stage_images.append(images)
                stage_slots.append(tuple(slots))
                images, slots = [], []

        packed = call(packed_kernel, struct(((groups - 1) * part, lanes + features)), (), messages)
        shared = [packed] + [share(packed, j) for j in range(1, sharers)]
        mine, out_mine = call(
            functools.partial(gathered_kernel, (groups, rows, sharers, devices, 3 * width)),
            [struct((groups * rows, lanes)), struct((groups * rows, features))],
            (),
            (own_block, w_out, *shared),
            [pltpu.VMEM(((groups - 1) * rows, lanes + features), F32)],
        )
        other, out_other = swap(mine), swap(out_mine)
        join = functools.partial(joined_kernel, (groups, members, rows))
        weights = call(join, struct((features, lanes)), (), (mine, other))
        table = sum(
            x[k * rows : k * rows + devices, 3 * width : 3 * width + devices].astype(F32)
            for x in (mine, other)
            for k in range(groups)
        )
        out_weights = lambda: call(join, struct((features, features)), (), (out_mine, out_other))
    else:
        gather = lambda x: lax.all_gather(x, "shard", axis=0, tiled=True)
        own = lax.axis_index("shard") // members
        columns = lambda w: lax.dynamic_slice_in_dim(gather(w), own * width, width, 1)
        weights = jnp.concatenate([columns(w) for w in (w_key, w_value, w_query)], axis=1)
        table = call(table_kernel, struct((round_up(devices, 16), 128)), small, ())
        table = jnp.sum(gather(table[None])[:, :devices, :devices].astype(F32), axis=0)
        normed = call(norm_kernel, struct((length, features)), (), (tokens[0], norm_gain))
        every = gather(normed[None])
        stage_images.append([every[i] for i in range(devices)])
        stage_slots.append(tuple((None, i) for i in range(devices)))
        out_weights = lambda: gather(w_out)

    state_shapes = (
        struct((devices, length, width)),
        struct((devices, width, length)),
        struct((groups, width, heads * length)),
        struct((groups, max(heads // 2, 1), 2 * HEAD_DIM, 2 * length), F32),
        struct((groups, HEAD_DIM, length), F32),
    )
    part_shapes = tuple(struct((length // 2, 2 * width)) for _ in range(groups))
    state = ()
    stages = len(stage_images)
    bounds = [-1] + [1 if s < stages - 1 else groups for s in range(stages)]
    for s in range(stages):
        last = s == stages - 1
        cfg = (groups, members, heads, bounds[s], bounds[s + 1], stage_slots[s], last)
        scratch = [pltpu.VMEM((groups, members * length, features), BF16), pltpu.SMEM((groups * devices + 1,), jnp.int32)]
        if last:
            scratch = [pltpu.VMEM(x.shape, x.dtype) for x in state_shapes] + scratch
        state = call(
            functools.partial(attention_kernel, cfg),
            part_shapes if last else state_shapes,
            (table,),
            (weights, *stage_images[s], *state),
            scratch,
            megabytes=24 if relayed else 60,
        )

    parts = [state[0]] + [exchange(state[k], k) for k in range(1, groups)]
    out = call(
        functools.partial(output_kernel, (groups, members)),
        struct((length, features)),
        (),
        (out_weights(), *parts),
        [pltpu.VMEM((groups, length, width), BF16)],
    )
    return out[None]


def solution(mesh):
    in_specs = (
        P(("group", "shard"), None, None),
        P(),
        P("shard", None),
        P("shard", None),
        P("shard", None),
        P("shard", None),
        P("group", None),
        P(("group", "shard"), None),
        P(("group", "shard")),
        P(("group", "shard"), None),
    )
    out_specs = P(("group", "shard"), None, None)
    return jax.shard_map(
        functools.partial(shards, dict(mesh.shape)),
        mesh=mesh,
        in_specs=in_specs,
        out_specs=out_specs,
        check_vma=False,
    )
```

profile of v0, /device:TPU:0, one launch (start us, length us, event | category | flops | bytes accessed | tf_op | source)
XLA Modules:
  0.0 69.1 jit_solution(6292477432502975944)
XLA Ops:
  0.7 2.8 %shard_map.100 = (bf16[192,768]{1,0:T(8,128)(2,1)}, bf16[96,640]{1,0:T(8,128)(2,1)}, bf16[24,1408]{1,0:T(8,128)(2,1)}, bf16[24,1408]{1,0:T(8,128)(2,1)}, bf16[24,1408]{1,0:T(8,128)(2,1)}) custom-call(s32[1,8]{1,0:T(1,128)} %refs_0_.1, s32[2,8]{1,0:T(2,128)} %bitcast.5, s32[1]{0:T(128)S(6)} %copy.11.refs_2_, s32[2,8]{1,0:T(2,128)} %bitcast.6, ...), custom_call_target="tpu_custom_call" | custom-call | tf_op jit(solution)/shard_map/pallas_call | solution.py:33
  4.0 4.5 %collective-permute-start.8 = (bf16[192,768]{1,0:T(8,128)(2,1)}, bf16[192,768]{1,0:T(8,128)(2,1)S(1)}, u32[]{:S(2)}, u32[]{:S(2)}) collective-permute-start(bf16[192,768]{1,0:T(8,128)(2,1)} %get-tuple-element.27.refs_2_), channel_id=1, source_target_pairs={{0,2},{2,4},{4,6},{3,1},{5,3},{7,5},{8,10},{10,12},{12,14},{11,9},... | collective-permute-start | bytes 884744 | tf_op jit(solution)/shard_map/ppermute | solution.py:349
  8.6 3.4 %collective-permute-start.11 = (bf16[192,768]{1,0:T(8,128)(2,1)S(1)}, bf16[192,768]{1,0:T(8,128)(2,1)S(1)}, u32[]{:S(2)}, u32[]{:S(2)}) collective-permute-start(bf16[192,768]{1,0:T(8,128)(2,1)S(1)} %collective-permute-done.10.refs_3_), channel_id=1, source_target_pairs={{0,2},{2,4},{4,6},{3,1},{5,3},{7,5},{8,10},{10,12},{12,14},{11,9},... | collective-permute-start | bytes 884744 | tf_op jit(solution)/shard_map/ppermute | solution.py:349
  12.0 1.7 %collective-permute-start = (bf16[24,1408]{1,0:T(8,128)(2,1)}, bf16[24,1408]{1,0:T(8,128)(2,1)S(1)}, u32[]{:S(2)}, u32[]{:S(2)}) collective-permute-start(bf16[24,1408]{1,0:T(8,128)(2,1)} %get-tuple-element.22), channel_id=1, source_target_pairs={{0,2},{1,3},{2,0},{3,1},{4,6},{5,7},{6,4},{7,5},{8,10},{9,11},{10,... | collective-permute-start | bytes 202760 | tf_op jit(solution)/shard_map/ppermute | solution.py:319
  13.7 2.7 %collective-permute-start.2 = (bf16[24,1408]{1,0:T(8,128)(2,1)}, bf16[24,1408]{1,0:T(8,128)(2,1)S(1)}, u32[]{:S(2)}, u32[]{:S(2)}) collective-permute-start(bf16[24,1408]{1,0:T(8,128)(2,1)} %get-tuple-element.24), channel_id=1, source_target_pairs={{0,6},{1,7},{2,4},{3,5},{4,2},{5,3},{6,0},{7,1},{8,14},{9,15},{10,... | collective-permute-start | bytes 202760 | tf_op jit(solution)/shard_map/ppermute | solution.py:319
  16.5 2.7 %collective-permute-done.refs_0_ = bf16[24,1408]{1,0:T(8,128)(2,1)S(1)} collective-permute-done((bf16[24,1408]{1,0:T(8,128)(2,1)}, bf16[24,1408]{1,0:T(8,128)(2,1)S(1)}, u32[]{:S(2)}, u32[]{:S(2)}) %collective-permute-start) | collective-permute-done | bytes 67616 | tf_op jit(solution)/shard_map/ppermute | solution.py:319
  19.2 2.0 %collective-permute-done.1.refs_1_ = bf16[24,1408]{1,0:T(8,128)(2,1)S(1)} collective-permute-done((bf16[24,1408]{1,0:T(8,128)(2,1)}, bf16[24,1408]{1,0:T(8,128)(2,1)S(1)}, u32[]{:S(2)}, u32[]{:S(2)}) %collective-permute-start.1) | collective-permute-done | bytes 67616 | tf_op jit(solution)/shard_map/ppermute | solution.py:319
  21.2 1.6 %collective-permute-start.3 = (bf16[72,1408]{1,0:T(8,128)(2,1)S(1)}, bf16[72,1408]{1,0:T(8,128)(2,1)S(1)}, u32[]{:S(2)}, u32[]{:S(2)}) collective-permute-start(bf16[72,1408]{1,0:T(8,128)(2,1)S(1)} %shard_map.101.refs_0_), channel_id=1, source_target_pairs={{0,8},{1,9},{2,10},{3,11},{4,12},{5,13},{6,14},{7,15},{8,0},{9,1},... | collective-permute-start | bytes 608264 | tf_op jit(solution)/shard_map/ppermute | solution.py:325
  22.8 1.5 %collective-permute-start.4 = (bf16[72,1408]{1,0:T(8,128)(2,1)S(1)}, bf16[72,1408]{1,0:T(8,128)(2,1)S(1)}, u32[]{:S(2)}, u32[]{:S(2)}) collective-permute-start(bf16[72,1408]{1,0:T(8,128)(2,1)S(1)} %shard_map.101.refs_0_), channel_id=1, source_target_pairs={{0,16},{1,17},{2,18},{3,19},{4,20},{5,21},{6,22},{7,23},{8,24},{9,... | collective-permute-start | bytes 608264 | tf_op jit(solution)/shard_map/ppermute | solution.py:325
  25.5 0.7 collective-permute-start.12
  26.2 2.4 %collective-permute-done.3.refs_1_ = bf16[72,1408]{1,0:T(8,128)(2,1)S(1)} collective-permute-done((bf16[72,1408]{1,0:T(8,128)(2,1)S(1)}, bf16[72,1408]{1,0:T(8,128)(2,1)S(1)}, u32[]{:S(2)}, u32[]{:S(2)}) %collective-permute-start.3) | collective-permute-done | bytes 202784 | tf_op jit(solution)/shard_map/ppermute | solution.py:325
  28.6 1.4 %collective-permute-start.19 = (bf16[192,768]{1,0:T(8,128)(2,1)S(1)}, bf16[192,768]{1,0:T(8,128)(2,1)S(1)}, u32[]{:S(2)}, u32[]{:S(2)}) collective-permute-start(bf16[192,768]{1,0:T(8,128)(2,1)S(1)} %collective-permute-done.8.refs_4_), channel_id=1, source_target_pairs={{0,1},{1,0},{2,3},{3,2},{4,5},{5,4},{6,7},{7,6},{8,9},{9,8},{10,11... | collective-permute-start | bytes 884744 | tf_op jit(solution)/shard_map/ppermute | solution.py:324
  29.9 4.8 %collective-permute-done.4.refs_2_ = bf16[72,1408]{1,0:T(8,128)(2,1)S(1)} collective-permute-done((bf16[72,1408]{1,0:T(8,128)(2,1)S(1)}, bf16[72,1408]{1,0:T(8,128)(2,1)S(1)}, u32[]{:S(2)}, u32[]{:S(2)}) %collective-permute-start.4) | collective-permute-done | bytes 202784 | tf_op jit(solution)/shard_map/ppermute | solution.py:325
  34.7 0.9 %copy-done.2 = bf16[96,640]{1,0:T(8,128)(2,1)S(1)} copy-done((bf16[96,640]{1,0:T(8,128)(2,1)S(1)}, bf16[96,640]{1,0:T(8,128)(2,1)}, u32[]{:S(2)}) %copy-start.2) | copy-done | bytes 122904
  37.8 1.5 %collective-permute-start.6 = (bf16[384,768]{1,0:T(8,128)(2,1)S(1)}, bf16[384,768]{1,0:T(8,128)(2,1)S(1)}, u32[]{:S(2)}, u32[]{:S(2)}) collective-permute-start(bf16[384,768]{1,0:T(8,128)(2,1)S(1)} %get-tuple-element.25.mine_ref), channel_id=1, source_target_pairs={{0,1},{1,0},{2,3},{3,2},{4,5},{5,4},{6,7},{7,6},{8,9},{9,8},{10,11... | collective-permute-start | bytes 1769480 | tf_op jit(solution)/shard_map/ppermute | solution.py:324
  39.8 4.3 %collective-permute-start.17 = (bf16[192,768]{1,0:T(8,128)(2,1)S(1)}, bf16[192,768]{1,0:T(8,128)(2,1)S(1)}, u32[]{:S(2)}, u32[]{:S(2)}) collective-permute-start(bf16[192,768]{1,0:T(8,128)(2,1)S(1)} %collective-permute-done.15.refs_6_), channel_id=1, source_target_pairs={{0,1},{1,0},{2,3},{3,2},{4,5},{5,4},{6,7},{7,6},{8,9},{9,8},{10,11... | collective-permute-start | bytes 884744 | tf_op jit(solution)/shard_map/ppermute | solution.py:324
  44.0 3.2 %collective-permute-start.18 = (bf16[192,768]{1,0:T(8,128)(2,1)S(1)}, bf16[192,768]{1,0:T(8,128)(2,1)S(1)}, u32[]{:S(2)}, u32[]{:S(2)}) collective-permute-start(bf16[192,768]{1,0:T(8,128)(2,1)S(1)} %collective-permute-done.16.refs_7_), channel_id=1, source_target_pairs={{0,1},{1,0},{2,3},{3,2},{4,5},{5,4},{6,7},{7,6},{8,9},{9,8},{10,11... | collective-permute-start | bytes 884744 | tf_op jit(solution)/shard_map/ppermute | solution.py:324
  47.4 4.3 %shard_map.105 = (bf16[8,192,192]{2,1,0:T(8,128)(2,1)S(1)}, bf16[8,192,192]{2,1,0:T(8,128)(2,1)S(1)}, bf16[4,192,576]{2,1,0:T(8,128)(2,1)S(1)}, f32[4,1,128,384]{3,2,1,0:T(8,128)S(1)}, f32[4,64,192]{2,1,0:T(8,128)S(1)}) custom-call(f32[8,8]{1,0:T(8,128)S(1)} %convert_add_fusion.refs_0_, bf16[768,640]{1,0:T(8,128)(2,1)S(1)} %shard_map.104.refs_1_, ...), custom_call_target="tpu_custom_call" | custom-call | tf_op jit(solution)/shard_map/pallas_call | solution.py:33
  51.7 6.7 %shard_map.106 = (bf16[96,384]{1,0:T(8,128)(2,1)S(1)}, bf16[96,384]{1,0:T(8,128)(2,1)S(1)}, bf16[96,384]{1,0:T(8,128)(2,1)S(1)}, bf16[96,384]{1,0:T(8,128)(2,1)S(1)}) custom-call(f32[8,8]{1,0:T(8,128)S(1)} %convert_add_fusion.refs_0_, bf16[768,640]{1,0:T(8,128)(2,1)S(1)} %shard_map.104.refs_1_, bf16[192,768]{1,0:T(8,128)(2,1)S(1)} %collective-permute-done.9.refs_2_, ...), custom_call_target="tpu_custom_call" | custom-call | tf_op jit(solution)/shard_map/pallas_call | solution.py:33
  58.5 1.9 %collective-permute-start.22 = (bf16[96,384]{1,0:T(8,128)(2,1)S(1)}, bf16[96,384]{1,0:T(8,128)(2,1)S(1)}, u32[]{:S(2)}, u32[]{:S(2)}) collective-permute-start(bf16[96,384]{1,0:T(8,128)(2,1)S(1)} %get-tuple-element.35), channel_id=1, source_target_pairs={{0,4},{1,5},{2,6},{3,7},{4,0},{5,1},{6,2},{7,3},{8,12},{9,13},{10,... | collective-permute-start | bytes 221192 | tf_op jit(solution)/shard_map/ppermute | solution.py:319
  60.4 2.5 %collective-permute-start.23 = (bf16[96,384]{1,0:T(8,128)(2,1)S(1)}, bf16[96,384]{1,0:T(8,128)(2,1)S(1)}, u32[]{:S(2)}, u32[]{:S(2)}) collective-permute-start(bf16[96,384]{1,0:T(8,128)(2,1)S(1)} %get-tuple-element.36), channel_id=1, source_target_pairs={{0,6},{1,7},{2,4},{3,5},{4,2},{5,3},{6,0},{7,1},{8,14},{9,15},{10,... | collective-permute-start | bytes 221192 | tf_op jit(solution)/shard_map/ppermute | solution.py:319
  63.0 0.7 %collective-permute-done.21.refs_2_ = bf16[96,384]{1,0:T(8,128)(2,1)S(1)} collective-permute-done((bf16[96,384]{1,0:T(8,128)(2,1)S(1)}, bf16[96,384]{1,0:T(8,128)(2,1)S(1)}, u32[]{:S(2)}, u32[]{:S(2)}) %collective-permute-start.21) | collective-permute-done | bytes 73760 | tf_op jit(solution)/shard_map/ppermute | solution.py:319
  63.7 4.1 %collective-permute-done.22.refs_3_ = bf16[96,384]{1,0:T(8,128)(2,1)S(1)} collective-permute-done((bf16[96,384]{1,0:T(8,128)(2,1)S(1)}, bf16[96,384]{1,0:T(8,128)(2,1)S(1)}, u32[]{:S(2)}, u32[]{:S(2)}) %collective-permute-start.22) | collective-permute-done | bytes 73760 | tf_op jit(solution)/shard_map/ppermute | solution.py:319
  67.8 1.3 %shard_map.107 = bf16[192,768]{1,0:T(8,128)(2,1)} custom-call(bf16[768,768]{1,0:T(8,128)(2,1)S(1)} %shard_map.103.refs_0_, bf16[96,384]{1,0:T(8,128)(2,1)S(1)} %get-tuple-element.33.refs_1_, bf16[96,384]{1,0:T(8,128)(2,1)S(1)} %collective-permute-done.21.refs_2_, bf16[96,384]{1,0:T(8,128)(2,1)S(1)} %collective-permute-done.22.refs_3_, ...), custom_call_target="tpu_custom_call" | custom-call | tf_op jit(solution)/shard_map/pallas_call | solution.py:33
  (39 shorter events, 4.8 us)
Async XLA Ops:
  3.5 5.1 %collective-permute-start.10 = (bf16[192,768]{1,0:T(8,128)(2,1)}, bf16[192,768]{1,0:T(8,128)(2,1)S(1)}, u32[]{:S(2)}, u32[]{:S(2)}) collective-permute-start(bf16[192,768]{1,0:T(8,128)(2,1)} %get-tuple-element.27.refs_2_), channel_id=1, source_target_pairs={{0,1},{1,0},{2,3},{3,2},{4,5},{5,4},{6,7},{7,6},{8,9},{9,8},{10,11... | collective-permute-start | bytes 884744 | tf_op jit(solution)/shard_map/ppermute | solution.py:324
  4.0 20.7 %collective-permute-start.8 = (bf16[192,768]{1,0:T(8,128)(2,1)}, bf16[192,768]{1,0:T(8,128)(2,1)S(1)}, u32[]{:S(2)}, u32[]{:S(2)}) collective-permute-start(bf16[192,768]{1,0:T(8,128)(2,1)} %get-tuple-element.27.refs_2_), channel_id=1, source_target_pairs={{0,2},{2,4},{4,6},{3,1},{5,3},{7,5},{8,10},{10,12},{12,14},{11,9},... | collective-permute-start | bytes 884744 | tf_op jit(solution)/shard_map/ppermute | solution.py:349
  8.6 16.9 %collective-permute-start.11 = (bf16[192,768]{1,0:T(8,128)(2,1)S(1)}, bf16[192,768]{1,0:T(8,128)(2,1)S(1)}, u32[]{:S(2)}, u32[]{:S(2)}) collective-permute-start(bf16[192,768]{1,0:T(8,128)(2,1)S(1)} %collective-permute-done.10.refs_3_), channel_id=1, source_target_pairs={{0,2},{2,4},{4,6},{3,1},{5,3},{7,5},{8,10},{10,12},{12,14},{11,9},... | collective-permute-start | bytes 884744 | tf_op jit(solution)/shard_map/ppermute | solution.py:349
  12.0 7.2 %collective-permute-start = (bf16[24,1408]{1,0:T(8,128)(2,1)}, bf16[24,1408]{1,0:T(8,128)(2,1)S(1)}, u32[]{:S(2)}, u32[]{:S(2)}) collective-permute-start(bf16[24,1408]{1,0:T(8,128)(2,1)} %get-tuple-element.22), channel_id=1, source_target_pairs={{0,2},{1,3},{2,0},{3,1},{4,6},{5,7},{6,4},{7,5},{8,10},{9,11},{10,... | collective-permute-start | bytes 202760 | tf_op jit(solution)/shard_map/ppermute | solution.py:319
  13.7 7.5 %collective-permute-start.1 = (bf16[24,1408]{1,0:T(8,128)(2,1)}, bf16[24,1408]{1,0:T(8,128)(2,1)S(1)}, u32[]{:S(2)}, u32[]{:S(2)}) collective-permute-start(bf16[24,1408]{1,0:T(8,128)(2,1)} %get-tuple-element.23), channel_id=1, source_target_pairs={{0,4},{1,5},{2,6},{3,7},{4,0},{5,1},{6,2},{7,3},{8,12},{9,13},{10,... | collective-permute-start | bytes 202760 | tf_op jit(solution)/shard_map/ppermute | solution.py:319
  13.7 7.5 %collective-permute-start.2 = (bf16[24,1408]{1,0:T(8,128)(2,1)}, bf16[24,1408]{1,0:T(8,128)(2,1)S(1)}, u32[]{:S(2)}, u32[]{:S(2)}) collective-permute-start(bf16[24,1408]{1,0:T(8,128)(2,1)} %get-tuple-element.24), channel_id=1, source_target_pairs={{0,6},{1,7},{2,4},{3,5},{4,2},{5,3},{6,0},{7,1},{8,14},{9,15},{10,... | collective-permute-start | bytes 202760 | tf_op jit(solution)/shard_map/ppermute | solution.py:319
  21.2 7.3 %collective-permute-start.3 = (bf16[72,1408]{1,0:T(8,128)(2,1)S(1)}, bf16[72,1408]{1,0:T(8,128)(2,1)S(1)}, u32[]{:S(2)}, u32[]{:S(2)}) collective-permute-start(bf16[72,1408]{1,0:T(8,128)(2,1)S(1)} %shard_map.101.refs_0_), channel_id=1, source_target_pairs={{0,8},{1,9},{2,10},{3,11},{4,12},{5,13},{6,14},{7,15},{8,0},{9,1},... | collective-permute-start | bytes 608264 | tf_op jit(solution)/shard_map/ppermute | solution.py:325
  22.8 11.9 %collective-permute-start.4 = (bf16[72,1408]{1,0:T(8,128)(2,1)S(1)}, bf16[72,1408]{1,0:T(8,128)(2,1)S(1)}, u32[]{:S(2)}, u32[]{:S(2)}) collective-permute-start(bf16[72,1408]{1,0:T(8,128)(2,1)S(1)} %shard_map.101.refs_0_), channel_id=1, source_target_pairs={{0,16},{1,17},{2,18},{3,19},{4,20},{5,21},{6,22},{7,23},{8,24},{9,... | collective-permute-start | bytes 608264 | tf_op jit(solution)/shard_map/ppermute | solution.py:325
  24.3 10.4 %collective-permute-start.5 = (bf16[72,1408]{1,0:T(8,128)(2,1)S(1)}, bf16[72,1408]{1,0:T(8,128)(2,1)S(1)}, u32[]{:S(2)}, u32[]{:S(2)}) collective-permute-start(bf16[72,1408]{1,0:T(8,128)(2,1)S(1)} %shard_map.101.refs_0_), channel_id=1, source_target_pairs={{0,24},{1,25},{2,26},{3,27},{4,28},{5,29},{6,30},{7,31},{8,16},{9,... | collective-permute-start | bytes 608264 | tf_op jit(solution)/shard_map/ppermute | solution.py:325
  24.8 11.6 %collective-permute-start.9 = (bf16[192,768]{1,0:T(8,128)(2,1)S(1)}, bf16[192,768]{1,0:T(8,128)(2,1)S(1)}, u32[]{:S(2)}, u32[]{:S(2)}) collective-permute-start(bf16[192,768]{1,0:T(8,128)(2,1)S(1)} %collective-permute-done.8.refs_4_), channel_id=1, source_target_pairs={{2,4},{4,6},{3,1},{5,3},{10,12},{12,14},{11,9},{13,11},{18,20},{20... | collective-permute-start | bytes 884744 | tf_op jit(solution)/shard_map/ppermute | solution.py:349
  25.5 11.6 %collective-permute-start.12 = (bf16[192,768]{1,0:T(8,128)(2,1)S(1)}, bf16[192,768]{1,0:T(8,128)(2,1)S(1)}, u32[]{:S(2)}, u32[]{:S(2)}) collective-permute-start(bf16[192,768]{1,0:T(8,128)(2,1)S(1)} %collective-permute-done.11.refs_5_), channel_id=1, source_target_pairs={{2,4},{4,6},{3,1},{5,3},{10,12},{12,14},{11,9},{13,11},{18,20},{20... | collective-permute-start | bytes 884744 | tf_op jit(solution)/shard_map/ppermute | solution.py:349
  28.6 9.2 %collective-permute-start.19 = (bf16[192,768]{1,0:T(8,128)(2,1)S(1)}, bf16[192,768]{1,0:T(8,128)(2,1)S(1)}, u32[]{:S(2)}, u32[]{:S(2)}) collective-permute-start(bf16[192,768]{1,0:T(8,128)(2,1)S(1)} %collective-permute-done.8.refs_4_), channel_id=1, source_target_pairs={{0,1},{1,0},{2,3},{3,2},{4,5},{5,4},{6,7},{7,6},{8,9},{9,8},{10,11... | collective-permute-start | bytes 884744 | tf_op jit(solution)/shard_map/ppermute | solution.py:324
  35.8 3.4 %collective-permute-start.7 = (bf16[384,640]{1,0:T(8,128)(2,1)S(1)}, bf16[384,640]{1,0:T(8,128)(2,1)S(1)}, u32[]{:S(2)}, u32[]{:S(2)}) collective-permute-start(bf16[384,640]{1,0:T(8,128)(2,1)S(1)} %get-tuple-element.26.mine_ref), channel_id=1, source_target_pairs={{0,1},{1,0},{2,3},{3,2},{4,5},{5,4},{6,7},{7,6},{8,9},{9,8},{10,11... | collective-permute-start | bytes 1474568 | tf_op jit(solution)/shard_map/ppermute | solution.py:324
  36.1 3.3 %collective-permute-start.20 = (bf16[192,768]{1,0:T(8,128)(2,1)S(1)}, bf16[192,768]{1,0:T(8,128)(2,1)S(1)}, u32[]{:S(2)}, u32[]{:S(2)}) collective-permute-start(bf16[192,768]{1,0:T(8,128)(2,1)S(1)} %collective-permute-done.11.refs_5_), channel_id=1, source_target_pairs={{0,1},{1,0},{2,3},{3,2},{4,5},{5,4},{6,7},{7,6},{8,9},{9,8},{10,11... | collective-permute-start | bytes 884744 | tf_op jit(solution)/shard_map/ppermute | solution.py:324
  36.4 3.4 %collective-permute-start.15 = (bf16[192,768]{1,0:T(8,128)(2,1)S(1)}, bf16[192,768]{1,0:T(8,128)(2,1)S(1)}, u32[]{:S(2)}, u32[]{:S(2)}) collective-permute-start(bf16[192,768]{1,0:T(8,128)(2,1)S(1)} %collective-permute-done.9.refs_2_), channel_id=1, source_target_pairs={{4,6},{3,1},{12,14},{11,9},{20,22},{19,17},{28,30},{27,25}} | collective-permute-start | bytes 884744 | tf_op jit(solution)/shard_map/ppermute | solution.py:349
  37.1 6.9 %collective-permute-start.16 = (bf16[192,768]{1,0:T(8,128)(2,1)S(1)}, bf16[192,768]{1,0:T(8,128)(2,1)S(1)}, u32[]{:S(2)}, u32[]{:S(2)}) collective-permute-start(bf16[192,768]{1,0:T(8,128)(2,1)S(1)} %collective-permute-done.12.refs_3_), channel_id=1, source_target_pairs={{4,6},{3,1},{12,14},{11,9},{20,22},{19,17},{28,30},{27,25}} | collective-permute-start | bytes 884744 | tf_op jit(solution)/shard_map/ppermute | solution.py:349
  37.8 25.1 %collective-permute-start.6 = (bf16[384,768]{1,0:T(8,128)(2,1)S(1)}, bf16[384,768]{1,0:T(8,128)(2,1)S(1)}, u32[]{:S(2)}, u32[]{:S(2)}) collective-permute-start(bf16[384,768]{1,0:T(8,128)(2,1)S(1)} %get-tuple-element.25.mine_ref), channel_id=1, source_target_pairs={{0,1},{1,0},{2,3},{3,2},{4,5},{5,4},{6,7},{7,6},{8,9},{9,8},{10,11... | collective-permute-start | bytes 1769480 | tf_op jit(solution)/shard_map/ppermute | solution.py:324
  39.2 12.4 %collective-permute-start.13 = (bf16[192,768]{1,0:T(8,128)(2,1)S(1)}, bf16[192,768]{1,0:T(8,128)(2,1)S(1)}, u32[]{:S(2)}, u32[]{:S(2)}) collective-permute-start(bf16[192,768]{1,0:T(8,128)(2,1)S(1)} %collective-permute-done.9.refs_2_), channel_id=1, source_target_pairs={{0,1},{1,0},{2,3},{3,2},{4,5},{5,4},{6,7},{7,6},{8,9},{9,8},{10,11... | collective-permute-start | bytes 884744 | tf_op jit(solution)/shard_map/ppermute | solution.py:324
  39.3 12.3 %collective-permute-start.14 = (bf16[192,768]{1,0:T(8,128)(2,1)S(1)}, bf16[192,768]{1,0:T(8,128)(2,1)S(1)}, u32[]{:S(2)}, u32[]{:S(2)}) collective-permute-start(bf16[192,768]{1,0:T(8,128)(2,1)S(1)} %collective-permute-done.12.refs_3_), channel_id=1, source_target_pairs={{0,1},{1,0},{2,3},{3,2},{4,5},{5,4},{6,7},{7,6},{8,9},{9,8},{10,11... | collective-permute-start | bytes 884744 | tf_op jit(solution)/shard_map/ppermute | solution.py:324
  39.8 11.9 %collective-permute-start.17 = (bf16[192,768]{1,0:T(8,128)(2,1)S(1)}, bf16[192,768]{1,0:T(8,128)(2,1)S(1)}, u32[]{:S(2)}, u32[]{:S(2)}) collective-permute-start(bf16[192,768]{1,0:T(8,128)(2,1)S(1)} %collective-permute-done.15.refs_6_), channel_id=1, source_target_pairs={{0,1},{1,0},{2,3},{3,2},{4,5},{5,4},{6,7},{7,6},{8,9},{9,8},{10,11... | collective-permute-start | bytes 884744 | tf_op jit(solution)/shard_map/ppermute | solution.py:324
  44.0 7.7 %collective-permute-start.18 = (bf16[192,768]{1,0:T(8,128)(2,1)S(1)}, bf16[192,768]{1,0:T(8,128)(2,1)S(1)}, u32[]{:S(2)}, u32[]{:S(2)}) collective-permute-start(bf16[192,768]{1,0:T(8,128)(2,1)S(1)} %collective-permute-done.16.refs_7_), channel_id=1, source_target_pairs={{0,1},{1,0},{2,3},{3,2},{4,5},{5,4},{6,7},{7,6},{8,9},{9,8},{10,11... | collective-permute-start | bytes 884744 | tf_op jit(solution)/shard_map/ppermute | solution.py:324
  58.5 5.3 %collective-permute-start.21 = (bf16[96,384]{1,0:T(8,128)(2,1)S(1)}, bf16[96,384]{1,0:T(8,128)(2,1)S(1)}, u32[]{:S(2)}, u32[]{:S(2)}) collective-permute-start(bf16[96,384]{1,0:T(8,128)(2,1)S(1)} %get-tuple-element.34), channel_id=1, source_target_pairs={{0,2},{1,3},{2,0},{3,1},{4,6},{5,7},{6,4},{7,5},{8,10},{9,11},{10,... | collective-permute-start | bytes 221192 | tf_op jit(solution)/shard_map/ppermute | solution.py:319
  58.5 9.3 %collective-permute-start.22 = (bf16[96,384]{1,0:T(8,128)(2,1)S(1)}, bf16[96,384]{1,0:T(8,128)(2,1)S(1)}, u32[]{:S(2)}, u32[]{:S(2)}) collective-permute-start(bf16[96,384]{1,0:T(8,128)(2,1)S(1)} %get-tuple-element.35), channel_id=1, source_target_pairs={{0,4},{1,5},{2,6},{3,7},{4,0},{5,1},{6,2},{7,3},{8,12},{9,13},{10,... | collective-permute-start | bytes 221192 | tf_op jit(solution)/shard_map/ppermute | solution.py:319
  60.4 7.4 %collective-permute-start.23 = (bf16[96,384]{1,0:T(8,128)(2,1)S(1)}, bf16[96,384]{1,0:T(8,128)(2,1)S(1)}, u32[]{:S(2)}, u32[]{:S(2)}) collective-permute-start(bf16[96,384]{1,0:T(8,128)(2,1)S(1)} %get-tuple-element.36), channel_id=1, source_target_pairs={{0,6},{1,7},{2,4},{3,5},{4,2},{5,3},{6,0},{7,1},{8,14},{9,15},{10,... | collective-permute-start | bytes 221192 | tf_op jit(solution)/shard_map/ppermute | solution.py:319
  (3 other events, 47.1 us)
where the time goes:
time: 69.3 us; the launch traced here: 69.1 us
  starting transfers between devices  35 us (51%)
  waiting for transfers between devices  16.7 us (24%)
  Pallas kernels  15.5 us (22%)
  local copies, waits for them, and re-layouts  0.91 us (1%)
  between operations  0.88 us (1%)
    pallas_call x8, Pallas kernels, call(): pl.pallas_call(kernel, out_shape=tuple(out_shape) if many else out_shape,...  15.5 us
    ppermute x9, starting transfers between devices, device_step(): lax.ppermute(x, 'shard', [(i, i ^ 1) for i in range(devices)])  11.9 us
    ppermute x6, starting transfers between devices, device_step(): a, b = (lax.ppermute(a, 'shard', pairs), lax.ppermute(b, 'shard', pairs))  10.6 us
    ppermute x6, waiting for transfers between devices, device_step(): exchange = lambda x, k: lax.ppermute(x, 'shard', across(k))  9.52 us
    ppermute x6, starting transfers between devices, device_step(): exchange = lambda x, k: lax.ppermute(x, 'shard', across(k))  8.9 us
    ppermute x3, waiting for transfers between devices, device_step(): lax.ppermute(x, ('group', 'shard'), [(g * devices + i, (g ^ j) * devices...  7.17 us
    ppermute x3, starting transfers between devices, device_step(): lax.ppermute(x, ('group', 'shard'), [(g * devices + i, (g ^ j) * devices...  3.55 us
  transfers between devices with their start and end apart: 24, of which 6 were waited for; matrix products, arithmetic and copies ran while one was open for 0% of the time, Pallas kernels for 17%

commit v1 on v0

--- a/solution.py
+++ b/solution.py
@@ -11,6 +11,7 @@
 
 HEADS = 12
 HEAD_DIM = 64
+ONES = 16
 TOGETHER = 4
 
 F32 = jnp.float32
@@ -156,20 +157,27 @@
 
 
 def attention_kernel(cfg, *refs):
-    groups, members, heads, low, high, slots, last = cfg
+    groups, members, heads, reach, fresh, slots, near, sent, _ = cfg
+    low, high = reach
     refs = list(refs)
     take = lambda count: [refs.pop(0) for _ in range(count)]
     table_ref, weights = take(2)
     image_refs = take(len(slots))
     first = low < 0
     state_in = [] if first else take(5)
-    out_refs = take(groups) if last else []
-    key_ref, value_ref, query_ref, pair_ref, single_ref = take(5)
+    out_refs = take(len(sent))
+    if fresh:
+        key_ref, value_ref, query_ref = take(3)
+    else:
+        key_ref, value_ref, query_ref = state_in[:3]
+    pair_ref, single_ref = take(2)
     pictures, list_ref = take(2)
     images = groups * members
     own, member = places(members)
     width = heads * HEAD_DIM
-    length = image_refs[0].shape[0]
+    length = value_ref.shape[2]
+    paired = heads // 2
+    paired_rows = 2 * paired * HEAD_DIM
     ahead = 2 * member - 1
 
     for ref, (step, flip) in zip(image_refs, slots):
@@ -186,31 +194,39 @@
     if first:
         pair_ref[...] = jnp.zeros_like(pair_ref)
         single_ref[...] = jnp.zeros_like(single_ref)
+        value_ref[:, paired_rows : paired_rows + ONES, :] = jnp.ones((images, ONES, length), BF16)
     else:
-        for new, old in zip((key_ref, value_ref, query_ref, pair_ref, single_ref), state_in):
-            new[...] = old[...]
+        new = (key_ref, value_ref, query_ref, pair_ref, single_ref)
+        for into, old in list(zip(new, state_in))[0 if fresh else 3 :]:
+            into[...] = old[...]
 
     count = jnp.int32(0)
     for place in range(groups):
+        apart = jnp.bitwise_xor(own, place)
         for target in range(images):
             away = jnp.maximum(jnp.abs(place - own), jnp.abs(target // members - own))
             amount = table_ref[place * members + member, target]
             list_ref[count] = place * images + target
-            count = count + ((amount > 0) & (away > low) & (away <= high)).astype(jnp.int32)
+            chosen = (amount > 0) & (away > low) & (away <= high) & (apart >= near[0]) & (apart < near[1])
+            count = count + chosen.astype(jnp.int32)
 
     def project(place, carry):
         away = jnp.abs(place - own)
 
         @pl.when((away > low) & (away <= high))
         def _():
+            rows_in = pictures[place, pl.ds(pl.multiple_of(member * length, 16), length), :]
             both = jnp.dot(pictures[place], weights[:, : 2 * width], preferred_element_type=F32).astype(BF16)
+            query = jnp.dot(rows_in, weights[:, 2 * width : 3 * width], preferred_element_type=F32).astype(BF16)
             aligned = width // 128 * 128
             for who in range(members):
+                image = place * members + who
                 rows = both[who * length : (who + 1) * length]
-                key_ref[place * members + who] = rows[:, :width]
-                value_ref[place * members + who] = rows[:, aligned:].T[width - aligned :]
-            rows = pictures[place, pl.ds(pl.multiple_of(member * length, 16), length), :]
-            query = jnp.dot(rows, weights[:, 2 * width : 3 * width], preferred_element_type=F32).astype(BF16)
+                key_ref[image] = rows[:, :width]
+                flipped = rows[:, aligned:].T[width - aligned :]
+                value_ref[image, :paired_rows] = flipped[:paired_rows]
+                if heads % 2:
+                    value_ref[image, paired_rows + ONES :] = flipped[paired_rows:]
             flipped = query.T
             head = lax.broadcasted_iota(jnp.int32, flipped.shape, 0) // HEAD_DIM
             for h in range(heads):
@@ -220,10 +236,10 @@
 
         return carry
 
-    lax.fori_loop(0, groups, project, 0)
+    if fresh:
+        lax.fori_loop(0, groups, project, 0)
 
     scale = math.log2(math.e) / math.sqrt(HEAD_DIM)
-    paired = heads // 2
 
     def block(number, carry):
         entries = []
@@ -235,23 +251,25 @@
             amount = jnp.where(there, table_ref[place * members + member, target], 0.0)
             entries.append((place, target, amount))
         scores = [jnp.dot(key_ref[t], query_ref[s], preferred_element_type=F32) for s, t, _ in entries]
-        expos, factors = [], []
-        for each, (_, _, amount) in zip(scores, entries):
+        expos = []
+        for each in scores:
             largest = jnp.max(each, axis=0, keepdims=True)
-            expo = jnp.exp2((each - largest) * scale)
-            total = jnp.sum(expo, axis=0, keepdims=True)
-            expos.append(expo.astype(BF16))
-            factors.append(amount / total)
+            expos.append(jnp.exp2((each - largest) * scale).astype(BF16))
         parts = []
-        for (_, target, _), expo, factor in zip(entries, expos, factors):
+        for (_, target, amount), expo in zip(entries, expos):
+            values = value_ref[target]
             for j in range(paired):
-                rows, lanes = slice(2 * j * HEAD_DIM, 2 * (j + 1) * HEAD_DIM), slice(2 * j * length, 2 * (j + 1) * length)
-                part = jnp.dot(value_ref[target, rows, :], expo[:, lanes], preferred_element_type=F32)
-                parts.append(part * factor[:, lanes])
+                lanes = slice(2 * j * length, 2 * (j + 1) * length)
+                rows = values[2 * j * HEAD_DIM : 2 * (j + 1) * HEAD_DIM]
+                if j == paired - 1:
+                    rows = values[2 * j * HEAD_DIM : paired_rows + ONES]
+                else:
+                    rows = jnp.concatenate([rows, values[paired_rows : paired_rows + ONES]], axis=0)
+                part = jnp.dot(rows, expo[:, lanes], preferred_element_type=F32)
+                parts.append(part[: 2 * HEAD_DIM] * (amount / part[2 * HEAD_DIM : 2 * HEAD_DIM + 1]))
             if heads % 2:
-                rows, lanes = slice((heads - 1) * HEAD_DIM, None), slice((heads - 1) * length, None)
-                part = jnp.dot(value_ref[target, rows, :], expo[:, lanes], preferred_element_type=F32)
-                parts.append(part * factor[:, lanes])
+                part = jnp.dot(values[paired_rows:], expo[:, (heads - 1) * length :], preferred_element_type=F32)
+                parts.append(part[ONES:] * (amount / part[:1]))
         for place, _, _ in entries:
             for j in range(paired):
                 pair_ref[place, j] += parts.pop(0)
@@ -261,25 +279,24 @@
 
     lax.fori_loop(0, (count + TOGETHER - 1) // TOGETHER, block, 0)
 
-    if last:
-        for k in range(groups):
-            place = jnp.bitwise_xor(own, k)
-            total = jnp.float32(1.0)
-            for target in range(images):
-                total += table_ref[place * members + member, target]
-            pieces = []
-            for h in range(heads):
-                if h == heads - 1 and heads % 2:
-                    pieces.append(single_ref[place])
-                else:
-                    at = h % 2
-                    pieces.append(
-                        pair_ref[place, h // 2, at * HEAD_DIM : (at + 1) * HEAD_DIM, at * length : (at + 1) * length]
-                    )
-            whole = (jnp.concatenate(pieces, axis=0) / total).astype(BF16).T
-            half = length // 2
-            out_refs[k][:, :width] = whole[:half]
-            out_refs[k][:, width:] = whole[half:]
+    for k, out_ref in zip(sent, out_refs):
+        place = jnp.bitwise_xor(own, k)
+        total = jnp.float32(1.0)
+        for target in range(images):
+            total += table_ref[place * members + member, target]
+        pieces = []
+        for h in range(heads):
+            if h == heads - 1 and heads % 2:
+                pieces.append(single_ref[place])
+            else:
+                at = h % 2
+                pieces.append(
+                    pair_ref[place, h // 2, at * HEAD_DIM : (at + 1) * HEAD_DIM, at * length : (at + 1) * length]
+                )
+        whole = (jnp.concatenate(pieces, axis=0) / total).astype(BF16).T
+        half = length // 2
+        out_ref[:, :width] = whole[:half]
+        out_ref[:, width:] = whole[half:]
 
 
 def output_kernel(cfg, *refs):
@@ -380,38 +397,49 @@
         table = call(table_kernel, struct((round_up(devices, 16), 128)), small, ())
         table = jnp.sum(gather(table[None])[:, :devices, :devices].astype(F32), axis=0)
         normed = call(norm_kernel, struct((length, features)), (), (tokens[0], norm_gain))
-        every = gather(normed[None])
-        stage_images.append([every[i] for i in range(devices)])
+        normed = gather(normed[None])
+        stage_images.append([normed[i] for i in range(devices)])
         stage_slots.append(tuple((None, i) for i in range(devices)))
         out_weights = lambda: gather(w_out)
 
     state_shapes = (
         struct((devices, length, width)),
-        struct((devices, width, length)),
+        struct((devices, width + ONES, length)),
         struct((groups, width, heads * length)),
         struct((groups, max(heads // 2, 1), 2 * HEAD_DIM, 2 * length), F32),
         struct((groups, HEAD_DIM, length), F32),
     )
-    part_shapes = tuple(struct((length // 2, 2 * width)) for _ in range(groups))
-    state = ()
-    stages = len(stage_images)
-    bounds = [-1] + [1 if s < stages - 1 else groups for s in range(stages)]
-    for s in range(stages):
-        last = s == stages - 1
-        cfg = (groups, members, heads, bounds[s], bounds[s + 1], stage_slots[s], last)
+    part_shape = struct((length // 2, 2 * width))
+    every = tuple(range(groups))
+    far, near = every[: groups // 2 - 1 : -1], every[: groups // 2]
+    if relayed:
+        stages = (
+            ((-1, 1), True, (0, groups), (), True),
+            ((1, groups), True, (0, groups), far + near, False),
+        )
+    else:
+        stages = (((-1, groups), True, (0, groups), every, False),)
+    parts, state = {}, ()
+    for s, (reach, fresh, asked, sent, keep) in enumerate(stages):
+        cfg = (groups, members, heads, reach, fresh, stage_slots[s], asked, sent, keep)
         scratch = [pltpu.VMEM((groups, members * length, features), BF16), pltpu.SMEM((groups * devices + 1,), jnp.int32)]
-        if last:
-            scratch = [pltpu.VMEM(x.shape, x.dtype) for x in state_shapes] + scratch
-        state = call(
+        shapes = [part_shape] * len(sent)
+        if keep:
+            shapes += state_shapes
+        else:
+            scratch = [pltpu.VMEM(x.shape, x.dtype) for x in state_shapes[0 if fresh else 3 :]] + scratch
+        results = call(
             functools.partial(attention_kernel, cfg),
-            part_shapes if last else state_shapes,
+            shapes,
             (table,),
             (weights, *stage_images[s], *state),
             scratch,
             megabytes=24 if relayed else 60,
         )
-
-    parts = [state[0]] + [exchange(state[k], k) for k in range(1, groups)]
+        for k, part in zip(sent, results):
+            parts[k] = exchange(part, k) if k else part
+        state = results[len(sent) :]
+    parts = [parts[k] for k in every]
     out = call(
         functools.partial(output_kernel, (groups, members)),
         struct((length, features)),

time: 69.3 us -> 68.4 us (0.987)
  Pallas kernels: 15.5 us -> 14.6 us
    pallas_call x8, Pallas kernels: 15.5 us -> 14.6 us  [call(): pl.pallas_call(kernel, out_shape=tuple(out_shape) if many else out_shape,...]
  transfers between devices with their start and end apart: 24 -> 24, of which waited for: 6 -> 6; matrix products, arithmetic and copies ran while one was open for 0% -> 0% of each run, Pallas kernels for 17% -> 15%
where the time goes in v1:
time: 68.4 us; the launch traced here: 68.2 us
  starting transfers between devices  35 us (51%)
  waiting for transfers between devices  16.7 us (24%)
  Pallas kernels  14.6 us (21%)
  local copies, waits for them, and re-layouts  0.91 us (1%)
  between operations  0.88 us (1%)
    pallas_call x8, Pallas kernels, call(): pl.pallas_call(kernel, out_shape=tuple(out_shape) if many else out_shape,...  14.6 us
    ppermute x9, starting transfers between devices, device_step(): lax.ppermute(x, 'shard', [(i, i ^ 1) for i in range(devices)])  11.9 us
    ppermute x6, starting transfers between devices, device_step(): a, b = (lax.ppermute(a, 'shard', pairs), lax.ppermute(b, 'shard', pairs))  10.6 us
    ppermute x6, waiting for transfers between devices, device_step(): exchange = lambda x, k: lax.ppermute(x, 'shard', across(k))  9.52 us
    ppermute x6, starting transfers between devices, device_step(): exchange = lambda x, k: lax.ppermute(x, 'shard', across(k))  8.9 us
    ppermute x3, waiting for transfers between devices, device_step(): lax.ppermute(x, ('group', 'shard'), [(g * devices + i, (g ^ j) * devices...  7.17 us
    ppermute x3, starting transfers between devices, device_step(): lax.ppermute(x, ('group', 'shard'), [(g * devices + i, (g ^ j) * devices...  3.55 us
  transfers between devices with their start and end apart: 24, of which 6 were waited for; matrix products, arithmetic and copies ran while one was open for 0% of the time, Pallas kernels for 15%

profile of v1, /device:TPU:0, one launch (start us, length us, event | category | flops | bytes accessed | tf_op | source)
XLA Modules:
  0.0 68.2 jit_solution(4402338532713026556)
XLA Ops:
  0.7 2.8 %shard_map.100 = (bf16[192,768]{1,0:T(8,128)(2,1)}, bf16[96,640]{1,0:T(8,128)(2,1)}, bf16[24,1408]{1,0:T(8,128)(2,1)}, bf16[24,1408]{1,0:T(8,128)(2,1)}, bf16[24,1408]{1,0:T(8,128)(2,1)}) custom-call(s32[1,8]{1,0:T(1,128)} %refs_0_.1, s32[2,8]{1,0:T(2,128)} %bitcast.5, s32[1]{0:T(128)S(6)} %copy.11.refs_2_, s32[2,8]{1,0:T(2,128)} %bitcast.6, ...), custom_call_target="tpu_custom_call" | custom-call | tf_op jit(solution)/shard_map/pallas_call | solution.py:34
  4.0 4.5 %collective-permute-start.8 = (bf16[192,768]{1,0:T(8,128)(2,1)}, bf16[192,768]{1,0:T(8,128)(2,1)S(1)}, u32[]{:S(2)}, u32[]{:S(2)}) collective-permute-start(bf16[192,768]{1,0:T(8,128)(2,1)} %get-tuple-element.27.refs_2_), channel_id=1, source_target_pairs={{0,2},{2,4},{4,6},{3,1},{5,3},{7,5},{8,10},{10,12},{12,14},{11,9},... | collective-permute-start | bytes 884744 | tf_op jit(solution)/shard_map/ppermute | solution.py:366
  8.6 3.4 %collective-permute-start.11 = (bf16[192,768]{1,0:T(8,128)(2,1)S(1)}, bf16[192,768]{1,0:T(8,128)(2,1)S(1)}, u32[]{:S(2)}, u32[]{:S(2)}) collective-permute-start(bf16[192,768]{1,0:T(8,128)(2,1)S(1)} %collective-permute-done.10.refs_3_), channel_id=1, source_target_pairs={{0,2},{2,4},{4,6},{3,1},{5,3},{7,5},{8,10},{10,12},{12,14},{11,9},... | collective-permute-start | bytes 884744 | tf_op jit(solution)/shard_map/ppermute | solution.py:366
  12.0 1.7 %collective-permute-start = (bf16[24,1408]{1,0:T(8,128)(2,1)}, bf16[24,1408]{1,0:T(8,128)(2,1)S(1)}, u32[]{:S(2)}, u32[]{:S(2)}) collective-permute-start(bf16[24,1408]{1,0:T(8,128)(2,1)} %get-tuple-element.22), channel_id=1, source_target_pairs={{0,2},{1,3},{2,0},{3,1},{4,6},{5,7},{6,4},{7,5},{8,10},{9,11},{10,... | collective-permute-start | bytes 202760 | tf_op jit(solution)/shard_map/ppermute | solution.py:336
  13.7 2.7 %collective-permute-start.2 = (bf16[24,1408]{1,0:T(8,128)(2,1)}, bf16[24,1408]{1,0:T(8,128)(2,1)S(1)}, u32[]{:S(2)}, u32[]{:S(2)}) collective-permute-start(bf16[24,1408]{1,0:T(8,128)(2,1)} %get-tuple-element.24), channel_id=1, source_target_pairs={{0,6},{1,7},{2,4},{3,5},{4,2},{5,3},{6,0},{7,1},{8,14},{9,15},{10,... | collective-permute-start | bytes 202760 | tf_op jit(solution)/shard_map/ppermute | solution.py:336
  16.5 2.7 %collective-permute-done.refs_0_ = bf16[24,1408]{1,0:T(8,128)(2,1)S(1)} collective-permute-done((bf16[24,1408]{1,0:T(8,128)(2,1)}, bf16[24,1408]{1,0:T(8,128)(2,1)S(1)}, u32[]{:S(2)}, u32[]{:S(2)}) %collective-permute-start) | collective-permute-done | bytes 67616 | tf_op jit(solution)/shard_map/ppermute | solution.py:336
  19.2 2.0 %collective-permute-done.1.refs_1_ = bf16[24,1408]{1,0:T(8,128)(2,1)S(1)} collective-permute-done((bf16[24,1408]{1,0:T(8,128)(2,1)}, bf16[24,1408]{1,0:T(8,128)(2,1)S(1)}, u32[]{:S(2)}, u32[]{:S(2)}) %collective-permute-start.1) | collective-permute-done | bytes 67616 | tf_op jit(solution)/shard_map/ppermute | solution.py:336
  21.2 1.6 %collective-permute-start.3 = (bf16[72,1408]{1,0:T(8,128)(2,1)S(1)}, bf16[72,1408]{1,0:T(8,128)(2,1)S(1)}, u32[]{:S(2)}, u32[]{:S(2)}) collective-permute-start(bf16[72,1408]{1,0:T(8,128)(2,1)S(1)} %shard_map.101.refs_0_), channel_id=1, source_target_pairs={{0,8},{1,9},{2,10},{3,11},{4,12},{5,13},{6,14},{7,15},{8,0},{9,1},... | collective-permute-start | bytes 608264 | tf_op jit(solution)/shard_map/ppermute | solution.py:342
  22.8 1.5 %collective-permute-start.4 = (bf16[72,1408]{1,0:T(8,128)(2,1)S(1)}, bf16[72,1408]{1,0:T(8,128)(2,1)S(1)}, u32[]{:S(2)}, u32[]{:S(2)}) collective-permute-start(bf16[72,1408]{1,0:T(8,128)(2,1)S(1)} %shard_map.101.refs_0_), channel_id=1, source_target_pairs={{0,16},{1,17},{2,18},{3,19},{4,20},{5,21},{6,22},{7,23},{8,24},{9,... | collective-permute-start | bytes 608264 | tf_op jit(solution)/shard_map/ppermute | solution.py:342
  25.5 0.7 collective-permute-start.12
  26.2 2.4 %collective-permute-done.3.refs_1_ = bf16[72,1408]{1,0:T(8,128)(2,1)S(1)} collective-permute-done((bf16[72,1408]{1,0:T(8,128)(2,1)S(1)}, bf16[72,1408]{1,0:T(8,128)(2,1)S(1)}, u32[]{:S(2)}, u32[]{:S(2)}) %collective-permute-start.3) | collective-permute-done | bytes 202784 | tf_op jit(solution)/shard_map/ppermute | solution.py:342
  28.6 1.4 %collective-permute-start.19 = (bf16[192,768]{1,0:T(8,128)(2,1)S(1)}, bf16[192,768]{1,0:T(8,128)(2,1)S(1)}, u32[]{:S(2)}, u32[]{:S(2)}) collective-permute-start(bf16[192,768]{1,0:T(8,128)(2,1)S(1)} %collective-permute-done.8.refs_4_), channel_id=1, source_target_pairs={{0,1},{1,0},{2,3},{3,2},{4,5},{5,4},{6,7},{7,6},{8,9},{9,8},{10,11... | collective-permute-start | bytes 884744 | tf_op jit(solution)/shard_map/ppermute | solution.py:341
  29.9 4.8 %collective-permute-done.4.refs_2_ = bf16[72,1408]{1,0:T(8,128)(2,1)S(1)} collective-permute-done((bf16[72,1408]{1,0:T(8,128)(2,1)S(1)}, bf16[72,1408]{1,0:T(8,128)(2,1)S(1)}, u32[]{:S(2)}, u32[]{:S(2)}) %collective-permute-start.4) | collective-permute-done | bytes 202784 | tf_op jit(solution)/shard_map/ppermute | solution.py:342
  34.7 0.9 %copy-done.2 = bf16[96,640]{1,0:T(8,128)(2,1)S(1)} copy-done((bf16[96,640]{1,0:T(8,128)(2,1)S(1)}, bf16[96,640]{1,0:T(8,128)(2,1)}, u32[]{:S(2)}) %copy-start.2) | copy-done | bytes 122904
  37.8 1.5 %collective-permute-start.6 = (bf16[384,768]{1,0:T(8,128)(2,1)S(1)}, bf16[384,768]{1,0:T(8,128)(2,1)S(1)}, u32[]{:S(2)}, u32[]{:S(2)}) collective-permute-start(bf16[384,768]{1,0:T(8,128)(2,1)S(1)} %get-tuple-element.25.mine_ref), channel_id=1, source_target_pairs={{0,1},{1,0},{2,3},{3,2},{4,5},{5,4},{6,7},{7,6},{8,9},{9,8},{10,11... | collective-permute-start | bytes 1769480 | tf_op jit(solution)/shard_map/ppermute | solution.py:341
  39.8 4.3 %collective-permute-start.17 = (bf16[192,768]{1,0:T(8,128)(2,1)S(1)}, bf16[192,768]{1,0:T(8,128)(2,1)S(1)}, u32[]{:S(2)}, u32[]{:S(2)}) collective-permute-start(bf16[192,768]{1,0:T(8,128)(2,1)S(1)} %collective-permute-done.15.refs_6_), channel_id=1, source_target_pairs={{0,1},{1,0},{2,3},{3,2},{4,5},{5,4},{6,7},{7,6},{8,9},{9,8},{10,11... | collective-permute-start | bytes 884744 | tf_op jit(solution)/shard_map/ppermute | solution.py:341
  44.0 3.2 %collective-permute-start.18 = (bf16[192,768]{1,0:T(8,128)(2,1)S(1)}, bf16[192,768]{1,0:T(8,128)(2,1)S(1)}, u32[]{:S(2)}, u32[]{:S(2)}) collective-permute-start(bf16[192,768]{1,0:T(8,128)(2,1)S(1)} %collective-permute-done.16.refs_7_), channel_id=1, source_target_pairs={{0,1},{1,0},{2,3},{3,2},{4,5},{5,4},{6,7},{7,6},{8,9},{9,8},{10,11... | collective-permute-start | bytes 884744 | tf_op jit(solution)/shard_map/ppermute | solution.py:341
  47.4 4.0 %shard_map.105 = (bf16[8,192,192]{2,1,0:T(8,128)(2,1)S(1)}, bf16[8,208,192]{2,1,0:T(8,128)(2,1)S(1)}, bf16[4,192,576]{2,1,0:T(8,128)(2,1)S(1)}, f32[4,1,128,384]{3,2,1,0:T(8,128)S(1)}, f32[4,64,192]{2,1,0:T(8,128)S(1)}) custom-call(f32[8,8]{1,0:T(8,128)S(1)} %convert_add_fusion.refs_0_, bf16[768,640]{1,0:T(8,128)(2,1)S(1)} %shard_map.104.refs_1_, ...), custom_call_target="tpu_custom_call" | custom-call | tf_op jit(solution)/shard_map/pallas_call | solution.py:34
  51.4 6.2 %shard_map.106 = (bf16[96,384]{1,0:T(8,128)(2,1)S(1)}, bf16[96,384]{1,0:T(8,128)(2,1)S(1)}, bf16[96,384]{1,0:T(8,128)(2,1)S(1)}, bf16[96,384]{1,0:T(8,128)(2,1)S(1)}) custom-call(f32[8,8]{1,0:T(8,128)S(1)} %convert_add_fusion.refs_0_, bf16[768,640]{1,0:T(8,128)(2,1)S(1)} %shard_map.104.refs_1_, bf16[192,768]{1,0:T(8,128)(2,1)S(1)} %collective-permute-done.9.refs_2_, ...), custom_call_target="tpu_custom_call" | custom-call | tf_op jit(solution)/shard_map/pallas_call | solution.py:34
  57.6 2.1 %collective-permute-start.22 = (bf16[96,384]{1,0:T(8,128)(2,1)S(1)}, bf16[96,384]{1,0:T(8,128)(2,1)S(1)}, u32[]{:S(2)}, u32[]{:S(2)}) collective-permute-start(bf16[96,384]{1,0:T(8,128)(2,1)S(1)} %get-tuple-element.35), channel_id=1, source_target_pairs={{0,4},{1,5},{2,6},{3,7},{4,0},{5,1},{6,2},{7,3},{8,12},{9,13},{10,... | collective-permute-start | bytes 221192 | tf_op jit(solution)/shard_map/ppermute | solution.py:336
  59.7 2.3 %collective-permute-start.23 = (bf16[96,384]{1,0:T(8,128)(2,1)S(1)}, bf16[96,384]{1,0:T(8,128)(2,1)S(1)}, u32[]{:S(2)}, u32[]{:S(2)}) collective-permute-start(bf16[96,384]{1,0:T(8,128)(2,1)S(1)} %get-tuple-element.36), channel_id=1, source_target_pairs={{0,6},{1,7},{2,4},{3,5},{4,2},{5,3},{6,0},{7,1},{8,14},{9,15},{10,... | collective-permute-start | bytes 221192 | tf_op jit(solution)/shard_map/ppermute | solution.py:336
  62.1 0.7 %collective-permute-done.21.refs_2_ = bf16[96,384]{1,0:T(8,128)(2,1)S(1)} collective-permute-done((bf16[96,384]{1,0:T(8,128)(2,1)S(1)}, bf16[96,384]{1,0:T(8,128)(2,1)S(1)}, u32[]{:S(2)}, u32[]{:S(2)}) %collective-permute-start.21) | collective-permute-done | bytes 73760 | tf_op jit(solution)/shard_map/ppermute | solution.py:336
  62.8 4.1 %collective-permute-done.22.refs_3_ = bf16[96,384]{1,0:T(8,128)(2,1)S(1)} collective-permute-done((bf16[96,384]{1,0:T(8,128)(2,1)S(1)}, bf16[96,384]{1,0:T(8,128)(2,1)S(1)}, u32[]{:S(2)}, u32[]{:S(2)}) %collective-permute-start.22) | collective-permute-done | bytes 73760 | tf_op jit(solution)/shard_map/ppermute | solution.py:336
  66.9 1.3 %shard_map.107 = bf16[192,768]{1,0:T(8,128)(2,1)} custom-call(bf16[768,768]{1,0:T(8,128)(2,1)S(1)} %shard_map.103.refs_0_, bf16[96,384]{1,0:T(8,128)(2,1)S(1)} %get-tuple-element.33.refs_1_, bf16[96,384]{1,0:T(8,128)(2,1)S(1)} %collective-permute-done.21.refs_2_, bf16[96,384]{1,0:T(8,128)(2,1)S(1)} %collective-permute-done.22.refs_3_, ...), custom_call_target="tpu_custom_call" | custom-call | tf_op jit(solution)/shard_map/pallas_call | solution.py:34
  (39 shorter events, 4.8 us)
Async XLA Ops:
  3.5 5.1 %collective-permute-start.10 = (bf16[192,768]{1,0:T(8,128)(2,1)}, bf16[192,768]{1,0:T(8,128)(2,1)S(1)}, u32[]{:S(2)}, u32[]{:S(2)}) collective-permute-start(bf16[192,768]{1,0:T(8,128)(2,1)} %get-tuple-element.27.refs_2_), channel_id=1, source_target_pairs={{0,1},{1,0},{2,3},{3,2},{4,5},{5,4},{6,7},{7,6},{8,9},{9,8},{10,11... | collective-permute-start | bytes 884744 | tf_op jit(solution)/shard_map/ppermute | solution.py:341
  4.0 20.7 %collective-permute-start.8 = (bf16[192,768]{1,0:T(8,128)(2,1)}, bf16[192,768]{1,0:T(8,128)(2,1)S(1)}, u32[]{:S(2)}, u32[]{:S(2)}) collective-permute-start(bf16[192,768]{1,0:T(8,128)(2,1)} %get-tuple-element.27.refs_2_), channel_id=1, source_target_pairs={{0,2},{2,4},{4,6},{3,1},{5,3},{7,5},{8,10},{10,12},{12,14},{11,9},... | collective-permute-start | bytes 884744 | tf_op jit(solution)/shard_map/ppermute | solution.py:366
  8.6 16.9 %collective-permute-start.11 = (bf16[192,768]{1,0:T(8,128)(2,1)S(1)}, bf16[192,768]{1,0:T(8,128)(2,1)S(1)}, u32[]{:S(2)}, u32[]{:S(2)}) collective-permute-start(bf16[192,768]{1,0:T(8,128)(2,1)S(1)} %collective-permute-done.10.refs_3_), channel_id=1, source_target_pairs={{0,2},{2,4},{4,6},{3,1},{5,3},{7,5},{8,10},{10,12},{12,14},{11,9},... | collective-permute-start | bytes 884744 | tf_op jit(solution)/shard_map/ppermute | solution.py:366
  12.0 7.2 %collective-permute-start = (bf16[24,1408]{1,0:T(8,128)(2,1)}, bf16[24,1408]{1,0:T(8,128)(2,1)S(1)}, u32[]{:S(2)}, u32[]{:S(2)}) collective-permute-start(bf16[24,1408]{1,0:T(8,128)(2,1)} %get-tuple-element.22), channel_id=1, source_target_pairs={{0,2},{1,3},{2,0},{3,1},{4,6},{5,7},{6,4},{7,5},{8,10},{9,11},{10,... | collective-permute-start | bytes 202760 | tf_op jit(solution)/shard_map/ppermute | solution.py:336
  13.7 7.5 %collective-permute-start.1 = (bf16[24,1408]{1,0:T(8,128)(2,1)}, bf16[24,1408]{1,0:T(8,128)(2,1)S(1)}, u32[]{:S(2)}, u32[]{:S(2)}) collective-permute-start(bf16[24,1408]{1,0:T(8,128)(2,1)} %get-tuple-element.23), channel_id=1, source_target_pairs={{0,4},{1,5},{2,6},{3,7},{4,0},{5,1},{6,2},{7,3},{8,12},{9,13},{10,... | collective-permute-start | bytes 202760 | tf_op jit(solution)/shard_map/ppermute | solution.py:336
  13.7 7.5 %collective-permute-start.2 = (bf16[24,1408]{1,0:T(8,128)(2,1)}, bf16[24,1408]{1,0:T(8,128)(2,1)S(1)}, u32[]{:S(2)}, u32[]{:S(2)}) collective-permute-start(bf16[24,1408]{1,0:T(8,128)(2,1)} %get-tuple-element.24), channel_id=1, source_target_pairs={{0,6},{1,7},{2,4},{3,5},{4,2},{5,3},{6,0},{7,1},{8,14},{9,15},{10,... | collective-permute-start | bytes 202760 | tf_op jit(solution)/shard_map/ppermute | solution.py:336
  21.2 7.3 %collective-permute-start.3 = (bf16[72,1408]{1,0:T(8,128)(2,1)S(1)}, bf16[72,1408]{1,0:T(8,128)(2,1)S(1)}, u32[]{:S(2)}, u32[]{:S(2)}) collective-permute-start(bf16[72,1408]{1,0:T(8,128)(2,1)S(1)} %shard_map.101.refs_0_), channel_id=1, source_target_pairs={{0,8},{1,9},{2,10},{3,11},{4,12},{5,13},{6,14},{7,15},{8,0},{9,1},... | collective-permute-start | bytes 608264 | tf_op jit(solution)/shard_map/ppermute | solution.py:342
  22.8 11.9 %collective-permute-start.4 = (bf16[72,1408]{1,0:T(8,128)(2,1)S(1)}, bf16[72,1408]{1,0:T(8,128)(2,1)S(1)}, u32[]{:S(2)}, u32[]{:S(2)}) collective-permute-start(bf16[72,1408]{1,0:T(8,128)(2,1)S(1)} %shard_map.101.refs_0_), channel_id=1, source_target_pairs={{0,16},{1,17},{2,18},{3,19},{4,20},{5,21},{6,22},{7,23},{8,24},{9,... | collective-permute-start | bytes 608264 | tf_op jit(solution)/shard_map/ppermute | solution.py:342
  24.3 10.4 %collective-permute-start.5 = (bf16[72,1408]{1,0:T(8,128)(2,1)S(1)}, bf16[72,1408]{1,0:T(8,128)(2,1)S(1)}, u32[]{:S(2)}, u32[]{:S(2)}) collective-permute-start(bf16[72,1408]{1,0:T(8,128)(2,1)S(1)} %shard_map.101.refs_0_), channel_id=1, source_target_pairs={{0,24},{1,25},{2,26},{3,27},{4,28},{5,29},{6,30},{7,31},{8,16},{9,... | collective-permute-start | bytes 608264 | tf_op jit(solution)/shard_map/ppermute | solution.py:342
  24.8 11.6 %collective-permute-start.9 = (bf16[192,768]{1,0:T(8,128)(2,1)S(1)}, bf16[192,768]{1,0:T(8,128)(2,1)S(1)}, u32[]{:S(2)}, u32[]{:S(2)}) collective-permute-start(bf16[192,768]{1,0:T(8,128)(2,1)S(1)} %collective-permute-done.8.refs_4_), channel_id=1, source_target_pairs={{2,4},{4,6},{3,1},{5,3},{10,12},{12,14},{11,9},{13,11},{18,20},{20... | collective-permute-start | bytes 884744 | tf_op jit(solution)/shard_map/ppermute | solution.py:366
  25.5 11.6 %collective-permute-start.12 = (bf16[192,768]{1,0:T(8,128)(2,1)S(1)}, bf16[192,768]{1,0:T(8,128)(2,1)S(1)}, u32[]{:S(2)}, u32[]{:S(2)}) collective-permute-start(bf16[192,768]{1,0:T(8,128)(2,1)S(1)} %collective-permute-done.11.refs_5_), channel_id=1, source_target_pairs={{2,4},{4,6},{3,1},{5,3},{10,12},{12,14},{11,9},{13,11},{18,20},{20... | collective-permute-start | bytes 884744 | tf_op jit(solution)/shard_map/ppermute | solution.py:366
  28.6 9.2 %collective-permute-start.19 = (bf16[192,768]{1,0:T(8,128)(2,1)S(1)}, bf16[192,768]{1,0:T(8,128)(2,1)S(1)}, u32[]{:S(2)}, u32[]{:S(2)}) collective-permute-start(bf16[192,768]{1,0:T(8,128)(2,1)S(1)} %collective-permute-done.8.refs_4_), channel_id=1, source_target_pairs={{0,1},{1,0},{2,3},{3,2},{4,5},{5,4},{6,7},{7,6},{8,9},{9,8},{10,11... | collective-permute-start | bytes 884744 | tf_op jit(solution)/shard_map/ppermute | solution.py:341
  35.8 3.4 %collective-permute-start.7 = (bf16[384,640]{1,0:T(8,128)(2,1)S(1)}, bf16[384,640]{1,0:T(8,128)(2,1)S(1)}, u32[]{:S(2)}, u32[]{:S(2)}) collective-permute-start(bf16[384,640]{1,0:T(8,128)(2,1)S(1)} %get-tuple-element.26.mine_ref), channel_id=1, source_target_pairs={{0,1},{1,0},{2,3},{3,2},{4,5},{5,4},{6,7},{7,6},{8,9},{9,8},{10,11... | collective-permute-start | bytes 1474568 | tf_op jit(solution)/shard_map/ppermute | solution.py:341
  36.1 3.3 %collective-permute-start.20 = (bf16[192,768]{1,0:T(8,128)(2,1)S(1)}, bf16[192,768]{1,0:T(8,128)(2,1)S(1)}, u32[]{:S(2)}, u32[]{:S(2)}) collective-permute-start(bf16[192,768]{1,0:T(8,128)(2,1)S(1)} %collective-permute-done.11.refs_5_), channel_id=1, source_target_pairs={{0,1},{1,0},{2,3},{3,2},{4,5},{5,4},{6,7},{7,6},{8,9},{9,8},{10,11... | collective-permute-start | bytes 884744 | tf_op jit(solution)/shard_map/ppermute | solution.py:341
  36.4 3.4 %collective-permute-start.15 = (bf16[192,768]{1,0:T(8,128)(2,1)S(1)}, bf16[192,768]{1,0:T(8,128)(2,1)S(1)}, u32[]{:S(2)}, u32[]{:S(2)}) collective-permute-start(bf16[192,768]{1,0:T(8,128)(2,1)S(1)} %collective-permute-done.9.refs_2_), channel_id=1, source_target_pairs={{4,6},{3,1},{12,14},{11,9},{20,22},{19,17},{28,30},{27,25}} | collective-permute-start | bytes 884744 | tf_op jit(solution)/shard_map/ppermute | solution.py:366
  37.1 6.9 %collective-permute-start.16 = (bf16[192,768]{1,0:T(8,128)(2,1)S(1)}, bf16[192,768]{1,0:T(8,128)(2,1)S(1)}, u32[]{:S(2)}, u32[]{:S(2)}) collective-permute-start(bf16[192,768]{1,0:T(8,128)(2,1)S(1)} %collective-permute-done.12.refs_3_), channel_id=1, source_target_pairs={{4,6},{3,1},{12,14},{11,9},{20,22},{19,17},{28,30},{27,25}} | collective-permute-start | bytes 884744 | tf_op jit(solution)/shard_map/ppermute | solution.py:366
  37.8 24.2 %collective-permute-start.6 = (bf16[384,768]{1,0:T(8,128)(2,1)S(1)}, bf16[384,768]{1,0:T(8,128)(2,1)S(1)}, u32[]{:S(2)}, u32[]{:S(2)}) collective-permute-start(bf16[384,768]{1,0:T(8,128)(2,1)S(1)} %get-tuple-element.25.mine_ref), channel_id=1, source_target_pairs={{0,1},{1,0},{2,3},{3,2},{4,5},{5,4},{6,7},{7,6},{8,9},{9,8},{10,11... | collective-permute-start | bytes 1769480 | tf_op jit(solution)/shard_map/ppermute | solution.py:341
  39.2 12.1 %collective-permute-start.13 = (bf16[192,768]{1,0:T(8,128)(2,1)S(1)}, bf16[192,768]{1,0:T(8,128)(2,1)S(1)}, u32[]{:S(2)}, u32[]{:S(2)}) collective-permute-start(bf16[192,768]{1,0:T(8,128)(2,1)S(1)} %collective-permute-done.9.refs_2_), channel_id=1, source_target_pairs={{0,1},{1,0},{2,3},{3,2},{4,5},{5,4},{6,7},{7,6},{8,9},{9,8},{10,11... | collective-permute-start | bytes 884744 | tf_op jit(solution)/shard_map/ppermute | solution.py:341
  39.3 12.0 %collective-permute-start.14 = (bf16[192,768]{1,0:T(8,128)(2,1)S(1)}, bf16[192,768]{1,0:T(8,128)(2,1)S(1)}, u32[]{:S(2)}, u32[]{:S(2)}) collective-permute-start(bf16[192,768]{1,0:T(8,128)(2,1)S(1)} %collective-permute-done.12.refs_3_), channel_id=1, source_target_pairs={{0,1},{1,0},{2,3},{3,2},{4,5},{5,4},{6,7},{7,6},{8,9},{9,8},{10,11... | collective-permute-start | bytes 884744 | tf_op jit(solution)/shard_map/ppermute | solution.py:341
  39.8 11.6 %collective-permute-start.17 = (bf16[192,768]{1,0:T(8,128)(2,1)S(1)}, bf16[192,768]{1,0:T(8,128)(2,1)S(1)}, u32[]{:S(2)}, u32[]{:S(2)}) collective-permute-start(bf16[192,768]{1,0:T(8,128)(2,1)S(1)} %collective-permute-done.15.refs_6_), channel_id=1, source_target_pairs={{0,1},{1,0},{2,3},{3,2},{4,5},{5,4},{6,7},{7,6},{8,9},{9,8},{10,11... | collective-permute-start | bytes 884744 | tf_op jit(solution)/shard_map/ppermute | solution.py:341
  44.0 7.3 %collective-permute-start.18 = (bf16[192,768]{1,0:T(8,128)(2,1)S(1)}, bf16[192,768]{1,0:T(8,128)(2,1)S(1)}, u32[]{:S(2)}, u32[]{:S(2)}) collective-permute-start(bf16[192,768]{1,0:T(8,128)(2,1)S(1)} %collective-permute-done.16.refs_7_), channel_id=1, source_target_pairs={{0,1},{1,0},{2,3},{3,2},{4,5},{5,4},{6,7},{7,6},{8,9},{9,8},{10,11... | collective-permute-start | bytes 884744 | tf_op jit(solution)/shard_map/ppermute | solution.py:341
  57.5 5.3 %collective-permute-start.21 = (bf16[96,384]{1,0:T(8,128)(2,1)S(1)}, bf16[96,384]{1,0:T(8,128)(2,1)S(1)}, u32[]{:S(2)}, u32[]{:S(2)}) collective-permute-start(bf16[96,384]{1,0:T(8,128)(2,1)S(1)} %get-tuple-element.34), channel_id=1, source_target_pairs={{0,2},{1,3},{2,0},{3,1},{4,6},{5,7},{6,4},{7,5},{8,10},{9,11},{10,... | collective-permute-start | bytes 221192 | tf_op jit(solution)/shard_map/ppermute | solution.py:336
  57.6 9.3 %collective-permute-start.22 = (bf16[96,384]{1,0:T(8,128)(2,1)S(1)}, bf16[96,384]{1,0:T(8,128)(2,1)S(1)}, u32[]{:S(2)}, u32[]{:S(2)}) collective-permute-start(bf16[96,384]{1,0:T(8,128)(2,1)S(1)} %get-tuple-element.35), channel_id=1, source_target_pairs={{0,4},{1,5},{2,6},{3,7},{4,0},{5,1},{6,2},{7,3},{8,12},{9,13},{10,... | collective-permute-start | bytes 221192 | tf_op jit(solution)/shard_map/ppermute | solution.py:336
  59.7 7.2 %collective-permute-start.23 = (bf16[96,384]{1,0:T(8,128)(2,1)S(1)}, bf16[96,384]{1,0:T(8,128)(2,1)S(1)}, u32[]{:S(2)}, u32[]{:S(2)}) collective-permute-start(bf16[96,384]{1,0:T(8,128)(2,1)S(1)} %get-tuple-element.36), channel_id=1, source_target_pairs={{0,6},{1,7},{2,4},{3,5},{4,2},{5,3},{6,0},{7,1},{8,14},{9,15},{10,... | collective-permute-start | bytes 221192 | tf_op jit(solution)/shard_map/ppermute | solution.py:336
  (3 other events, 47.1 us)

commit v2 on v1

--- a/solution.py
+++ b/solution.py
@@ -29,13 +29,13 @@
     return jax.ShapeDtypeStruct(shape, dtype)
 
 
-def call(kernel, out_shape, smem, vmem, scratch=(), megabytes=16, whole=()):
+def call(kernel, out_shape, smem, vmem, scratch=(), megabytes=16, whole=(), out_spec=VMEM_SPEC):
     many = isinstance(out_shape, (tuple, list))
     return pl.pallas_call(
         kernel,
         out_shape=tuple(out_shape) if many else out_shape,
         in_specs=[SMEM_SPEC] * len(smem) + [VMEM_SPEC] * len(vmem) + [HBM_SPEC] * len(whole),
-        out_specs=(VMEM_SPEC,) * len(out_shape) if many else VMEM_SPEC,
+        out_specs=(out_spec,) * len(out_shape) if many else out_spec,
         scratch_shapes=list(scratch),
         compiler_params=pltpu.CompilerParams(vmem_limit_bytes=megabytes * 1024 * 1024),
     )(*smem, *vmem, *whole)
@@ -68,44 +68,58 @@
 def message_kernel(cfg, *refs):
     groups, members, sharers = cfg
     sources, refs = refs[:10], refs[10:]
-    normed_ref, own_ref, message_refs, refs = refs[0], refs[1], refs[2 : 1 + groups], refs[1 + groups :]
-    copied, wide, sem = refs[:10], refs[10], refs[11]
-    owner_ref, pairs_ref, count_ref, conf_ref, query_ref, key_ref, value_ref, out_ref, tokens_ref, gain_ref = copied
-    copies = [pltpu.make_async_copy(source, into, sem.at[i]) for i, (source, into) in enumerate(zip(sources, copied))]
-    for each in copies:
-        each.start()
+    results, refs = refs[: 1 + groups], refs[1 + groups :]
+    small, whole, parts, made, (in_sem, out_sem) = refs[:4], refs[4:9], refs[9:13], refs[13:-2], refs[-2:]
+    owner_ref, pairs_ref, count_ref, conf_ref = small
+    tokens_ref, gain_ref = whole[3:]
+    normed_ref, own_ref, message_refs = made[0], made[1], made[2:]
     own, _ = places(members)
-    rows, features = query_ref.shape
+    rows, features = whole[0].shape
     width = features // groups
     part = rows // sharers
     start = pl.multiple_of(lax.axis_index("group") * part, 8)
+    key, value, query, out = (sources[i] for i in (5, 6, 4, 7))
+    moves = [(source, into) for source, into in zip(sources[:4], small)]
+    moves += [(source.at[pl.ds(start, part), :], into) for source, into in zip((key, value, query, out), parts)]
+    moves += [(source, into) for source, into in zip((key, value, query, sources[8], sources[9]), whole)]
+    moves = [pltpu.make_async_copy(source, into, in_sem.at[i]) for i, (source, into) in enumerate(moves)]
+    stores = [pltpu.make_async_copy(source, into, out_sem.at[i]) for i, (source, into) in enumerate(zip(made, results))]
+    for move in moves:
+        move.start()
+
     lanes = own_ref.shape[1]
-    for each in copies:
-        each.wait()
-    for i, ref in enumerate((key_ref, value_ref, query_ref, out_ref)):
-        wide[i] = ref[...].astype(F32)
-    for h in range(groups):
-        cut = slice(h * width, (h + 1) * width)
-
-        @pl.when(own == h)
-        def _(cut=cut):
-            for i, ref in enumerate((key_ref, value_ref, query_ref)):
-                own_ref[:, i * width : (i + 1) * width] = ref[:, cut]
-
-        for k in range(1, groups):
-
-            @pl.when(own == h ^ k)
-            def _(k=k, cut=cut):
-                for i in range(3):
-                    message_refs[k - 1][:, i * width : (i + 1) * width] = wide[i, pl.ds(start, part), cut].astype(BF16)
-
+    for move in moves[:8]:
+        move.wait()
     images = groups * members
     table = direction_table(owner_ref, pairs_ref, count_ref, conf_ref, (images, lanes - 3 * width)).astype(BF16)
+    for h in range(groups):
+        for k in range(1, groups):
+
+            @pl.when(own == h ^ k)
+            def _(k=k, cut=slice(h * width, (h + 1) * width)):
+                for i in range(3):
+                    message_refs[k - 1][:, i * width : (i + 1) * width] = parts[i][:, cut]
+
+    for ref in message_refs:
+        ref[:, lanes:] = parts[3][...]
+        ref[:images, 3 * width : lanes] = table
+    for store in stores[2:]:
+        store.start()
+    for move in moves[8:]:
+        move.wait()
+    normed_ref[...] = layer_norm(tokens_ref[...], gain_ref[...])
+    stores[0].start()
+    for h in range(groups):
+
+        @pl.when(own == h)
+        def _(cut=slice(h * width, (h + 1) * width)):
+            for i, ref in enumerate(whole[:3]):
+                own_ref[:, i * width : (i + 1) * width] = ref[:, cut]
+
     own_ref[:images, 3 * width :] = table
-    for ref in message_refs:
-        ref[:, lanes:] = wide[3, pl.ds(start, part), :].astype(BF16)
-        ref[:images, 3 * width : lanes] = table
-    normed_ref[...] = layer_norm(tokens_ref[...], gain_ref[...])
+    stores[1].start()
+    for store in stores:
+        store.wait()
 
 
 def layer_norm(tokens, gain):
@@ -345,16 +359,20 @@
             [(g * devices + i, (g ^ j) * devices + i) for g in range(sharers) for i in range(devices)],
         )
         arrays = (w_query, w_key, w_value, w_out, tokens[0], norm_gain)
+        made = [struct((length, features)), struct((rows, lanes))] + [struct((part, lanes + features))] * (groups - 1)
+        scratch = [pltpu.SMEM(x.shape, x.dtype) for x in small]
+        scratch += [pltpu.VMEM(x.shape, x.dtype) for x in (w_key, w_value, w_query, tokens[0], norm_gain)]
+        scratch += [pltpu.VMEM((part, features), BF16)] * 4 + [pltpu.VMEM(x.shape, x.dtype) for x in made]
+        scratch += [pltpu.SemaphoreType.DMA((13,)), pltpu.SemaphoreType.DMA((len(made),))]
         normed, own_block, *messages = call(
             functools.partial(message_kernel, (groups, members, sharers)),
-            [struct((length, features)), struct((rows, lanes))] + [struct((part, lanes + features))] * (groups - 1),
+            made,
             (),
             (),
-            [pltpu.SMEM(x.shape, x.dtype) for x in small]
-            + [pltpu.VMEM(x.shape, x.dtype) for x in arrays]
-            + [pltpu.VMEM((4, rows, features), F32), pltpu.SemaphoreType.DMA((10,))],
+            scratch,
             megabytes=62,
             whole=(*small, *arrays),
+            out_spec=HBM_SPEC,
         )
         messages = [exchange(messages[k - 1], k) for k in range(1, groups)]
         own_a, own_b = normed, swap(normed)

time: 68.4 us -> 68.1 us (level)
  transfers between devices with their start and end apart: 24 -> 24, of which waited for: 6 -> 6; matrix products, arithmetic and copies ran while one was open for 0% -> 0% of each run, Pallas kernels for 15% -> 16%
where the time goes in v2:
time: 68.1 us; the launch traced here: 67.8 us
  starting transfers between devices  35.2 us (52%)
  waiting for transfers between devices  16.5 us (24%)
  Pallas kernels  14.3 us (21%)
  local copies, waits for them, and re-layouts  0.91 us (1%)
  between operations  0.88 us (1%)
    pallas_call x8, Pallas kernels, call(): pl.pallas_call(kernel, out_shape=tuple(out_shape) if many else out_shape,...  14.3 us
    ppermute x9, starting transfers between devices, device_step(): lax.ppermute(x, 'shard', [(i, i ^ 1) for i in range(devices)])  12.1 us
    ppermute x6, starting transfers between devices, device_step(): a, b = (lax.ppermute(a, 'shard', pairs), lax.ppermute(b, 'shard', pairs))  10.7 us
    ppermute x6, waiting for transfers between devices, device_step(): exchange = lambda x, k: lax.ppermute(x, 'shard', across(k))  9.46 us
    ppermute x6, starting transfers between devices, device_step(): exchange = lambda x, k: lax.ppermute(x, 'shard', across(k))  8.9 us
    ppermute x3, waiting for transfers between devices, device_step(): lax.ppermute(x, ('group', 'shard'), [(g * devices + i, (g ^ j) * devices...  6.99 us
    ppermute x3, starting transfers between devices, device_step(): lax.ppermute(x, ('group', 'shard'), [(g * devices + i, (g ^ j) * devices...  3.55 us
  transfers between devices with their start and end apart: 24, of which 6 were waited for; matrix products, arithmetic and copies ran while one was open for 0% of the time, Pallas kernels for 16%

profile of v2, /device:TPU:0, one launch (start us, length us, event | category | flops | bytes accessed | tf_op | source)
XLA Modules:
  0.0 67.8 jit_solution(15749052287744242618)
XLA Ops:
  0.7 2.4 %shard_map.100 = (bf16[192,768]{1,0:T(8,128)(2,1)}, bf16[96,640]{1,0:T(8,128)(2,1)}, bf16[24,1408]{1,0:T(8,128)(2,1)}, bf16[24,1408]{1,0:T(8,128)(2,1)}, bf16[24,1408]{1,0:T(8,128)(2,1)}) custom-call(s32[1,8]{1,0:T(1,128)} %refs_0_.1, s32[2,8]{1,0:T(2,128)} %bitcast.5, s32[1]{0:T(128)S(6)} %copy.11.refs_2_, s32[2,8]{1,0:T(2,128)} %bitcast.6, ...), custom_call_target="tpu_custom_call" | custom-call | tf_op jit(solution)/shard_map/pallas_call | solution.py:34
  3.7 4.5 %collective-permute-start.8 = (bf16[192,768]{1,0:T(8,128)(2,1)}, bf16[192,768]{1,0:T(8,128)(2,1)S(1)}, u32[]{:S(2)}, u32[]{:S(2)}) collective-permute-start(bf16[192,768]{1,0:T(8,128)(2,1)} %get-tuple-element.27.refs_2_), channel_id=1, source_target_pairs={{0,2},{2,4},{4,6},{3,1},{5,3},{7,5},{8,10},{10,12},{12,14},{11,9},... | collective-permute-start | bytes 884744 | tf_op jit(solution)/shard_map/ppermute | solution.py:384
  8.2 3.5 %collective-permute-start.11 = (bf16[192,768]{1,0:T(8,128)(2,1)S(1)}, bf16[192,768]{1,0:T(8,128)(2,1)S(1)}, u32[]{:S(2)}, u32[]{:S(2)}) collective-permute-start(bf16[192,768]{1,0:T(8,128)(2,1)S(1)} %collective-permute-done.10.refs_3_), channel_id=1, source_target_pairs={{0,2},{2,4},{4,6},{3,1},{5,3},{7,5},{8,10},{10,12},{12,14},{11,9},... | collective-permute-start | bytes 884744 | tf_op jit(solution)/shard_map/ppermute | solution.py:384
  11.7 1.6 %collective-permute-start = (bf16[24,1408]{1,0:T(8,128)(2,1)}, bf16[24,1408]{1,0:T(8,128)(2,1)S(1)}, u32[]{:S(2)}, u32[]{:S(2)}) collective-permute-start(bf16[24,1408]{1,0:T(8,128)(2,1)} %get-tuple-element.22), channel_id=1, source_target_pairs={{0,2},{1,3},{2,0},{3,1},{4,6},{5,7},{6,4},{7,5},{8,10},{9,11},{10,... | collective-permute-start | bytes 202760 | tf_op jit(solution)/shard_map/ppermute | solution.py:350
  13.3 2.8 %collective-permute-start.2 = (bf16[24,1408]{1,0:T(8,128)(2,1)}, bf16[24,1408]{1,0:T(8,128)(2,1)S(1)}, u32[]{:S(2)}, u32[]{:S(2)}) collective-permute-start(bf16[24,1408]{1,0:T(8,128)(2,1)} %get-tuple-element.24), channel_id=1, source_target_pairs={{0,6},{1,7},{2,4},{3,5},{4,2},{5,3},{6,0},{7,1},{8,14},{9,15},{10,... | collective-permute-start | bytes 202760 | tf_op jit(solution)/shard_map/ppermute | solution.py:350
  16.2 2.6 %collective-permute-done.refs_0_ = bf16[24,1408]{1,0:T(8,128)(2,1)S(1)} collective-permute-done((bf16[24,1408]{1,0:T(8,128)(2,1)}, bf16[24,1408]{1,0:T(8,128)(2,1)S(1)}, u32[]{:S(2)}, u32[]{:S(2)}) %collective-permute-start) | collective-permute-done | bytes 67616 | tf_op jit(solution)/shard_map/ppermute | solution.py:350
  18.8 2.1 %collective-permute-done.1.refs_1_ = bf16[24,1408]{1,0:T(8,128)(2,1)S(1)} collective-permute-done((bf16[24,1408]{1,0:T(8,128)(2,1)}, bf16[24,1408]{1,0:T(8,128)(2,1)S(1)}, u32[]{:S(2)}, u32[]{:S(2)}) %collective-permute-start.1) | collective-permute-done | bytes 67616 | tf_op jit(solution)/shard_map/ppermute | solution.py:350
  20.9 1.6 %collective-permute-start.3 = (bf16[72,1408]{1,0:T(8,128)(2,1)S(1)}, bf16[72,1408]{1,0:T(8,128)(2,1)S(1)}, u32[]{:S(2)}, u32[]{:S(2)}) collective-permute-start(bf16[72,1408]{1,0:T(8,128)(2,1)S(1)} %shard_map.101.refs_0_), channel_id=1, source_target_pairs={{0,8},{1,9},{2,10},{3,11},{4,12},{5,13},{6,14},{7,15},{8,0},{9,1},... | collective-permute-start | bytes 608264 | tf_op jit(solution)/shard_map/ppermute | solution.py:356
  22.4 1.5 %collective-permute-start.4 = (bf16[72,1408]{1,0:T(8,128)(2,1)S(1)}, bf16[72,1408]{1,0:T(8,128)(2,1)S(1)}, u32[]{:S(2)}, u32[]{:S(2)}) collective-permute-start(bf16[72,1408]{1,0:T(8,128)(2,1)S(1)} %shard_map.101.refs_0_), channel_id=1, source_target_pairs={{0,16},{1,17},{2,18},{3,19},{4,20},{5,21},{6,22},{7,23},{8,24},{9,... | collective-permute-start | bytes 608264 | tf_op jit(solution)/shard_map/ppermute | solution.py:356
  25.1 0.7 %collective-permute-start.12 = (bf16[192,768]{1,0:T(8,128)(2,1)S(1)}, bf16[192,768]{1,0:T(8,128)(2,1)S(1)}, u32[]{:S(2)}, u32[]{:S(2)}) collective-permute-start(bf16[192,768]{1,0:T(8,128)(2,1)S(1)} %collective-permute-done.11.refs_5_), channel_id=1, source_target_pairs={{2,4},{4,6},{3,1},{5,3},{10,12},{12,14},{11,9},{13,11},{18,20},{20... | collective-permute-start | bytes 884744 | tf_op jit(solution)/shard_map/ppermute | solution.py:384
  25.8 2.4 %collective-permute-done.3.refs_1_ = bf16[72,1408]{1,0:T(8,128)(2,1)S(1)} collective-permute-done((bf16[72,1408]{1,0:T(8,128)(2,1)S(1)}, bf16[72,1408]{1,0:T(8,128)(2,1)S(1)}, u32[]{:S(2)}, u32[]{:S(2)}) %collective-permute-start.3) | collective-permute-done | bytes 202784 | tf_op jit(solution)/shard_map/ppermute | solution.py:356
  28.1 1.5 %collective-permute-start.19 = (bf16[192,768]{1,0:T(8,128)(2,1)S(1)}, bf16[192,768]{1,0:T(8,128)(2,1)S(1)}, u32[]{:S(2)}, u32[]{:S(2)}) collective-permute-start(bf16[192,768]{1,0:T(8,128)(2,1)S(1)} %collective-permute-done.8.refs_4_), channel_id=1, source_target_pairs={{0,1},{1,0},{2,3},{3,2},{4,5},{5,4},{6,7},{7,6},{8,9},{9,8},{10,11... | collective-permute-start | bytes 884744 | tf_op jit(solution)/shard_map/ppermute | solution.py:355
  29.6 4.6 %collective-permute-done.4.refs_2_ = bf16[72,1408]{1,0:T(8,128)(2,1)S(1)} collective-permute-done((bf16[72,1408]{1,0:T(8,128)(2,1)S(1)}, bf16[72,1408]{1,0:T(8,128)(2,1)S(1)}, u32[]{:S(2)}, u32[]{:S(2)}) %collective-permute-start.4) | collective-permute-done | bytes 202784 | tf_op jit(solution)/shard_map/ppermute | solution.py:356
  34.3 0.9 %copy-done.2 = bf16[96,640]{1,0:T(8,128)(2,1)S(1)} copy-done((bf16[96,640]{1,0:T(8,128)(2,1)S(1)}, bf16[96,640]{1,0:T(8,128)(2,1)}, u32[]{:S(2)}) %copy-start.2) | copy-done | bytes 122904
  37.4 1.5 %collective-permute-start.6 = (bf16[384,768]{1,0:T(8,128)(2,1)S(1)}, bf16[384,768]{1,0:T(8,128)(2,1)S(1)}, u32[]{:S(2)}, u32[]{:S(2)}) collective-permute-start(bf16[384,768]{1,0:T(8,128)(2,1)S(1)} %get-tuple-element.25.mine_ref), channel_id=1, source_target_pairs={{0,1},{1,0},{2,3},{3,2},{4,5},{5,4},{6,7},{7,6},{8,9},{9,8},{10,11... | collective-permute-start | bytes 1769480 | tf_op jit(solution)/shard_map/ppermute | solution.py:355
  39.4 4.3 %collective-permute-start.17 = (bf16[192,768]{1,0:T(8,128)(2,1)S(1)}, bf16[192,768]{1,0:T(8,128)(2,1)S(1)}, u32[]{:S(2)}, u32[]{:S(2)}) collective-permute-start(bf16[192,768]{1,0:T(8,128)(2,1)S(1)} %collective-permute-done.15.refs_6_), channel_id=1, source_target_pairs={{0,1},{1,0},{2,3},{3,2},{4,5},{5,4},{6,7},{7,6},{8,9},{9,8},{10,11... | collective-permute-start | bytes 884744 | tf_op jit(solution)/shard_map/ppermute | solution.py:355
  43.7 3.2 %collective-permute-start.18 = (bf16[192,768]{1,0:T(8,128)(2,1)S(1)}, bf16[192,768]{1,0:T(8,128)(2,1)S(1)}, u32[]{:S(2)}, u32[]{:S(2)}) collective-permute-start(bf16[192,768]{1,0:T(8,128)(2,1)S(1)} %collective-permute-done.16.refs_7_), channel_id=1, source_target_pairs={{0,1},{1,0},{2,3},{3,2},{4,5},{5,4},{6,7},{7,6},{8,9},{9,8},{10,11... | collective-permute-start | bytes 884744 | tf_op jit(solution)/shard_map/ppermute | solution.py:355
  47.0 4.0 %shard_map.105 = (bf16[8,192,192]{2,1,0:T(8,128)(2,1)S(1)}, bf16[8,208,192]{2,1,0:T(8,128)(2,1)S(1)}, bf16[4,192,576]{2,1,0:T(8,128)(2,1)S(1)}, f32[4,1,128,384]{3,2,1,0:T(8,128)S(1)}, f32[4,64,192]{2,1,0:T(8,128)S(1)}) custom-call(f32[8,8]{1,0:T(8,128)S(1)} %convert_add_fusion.refs_0_, bf16[768,640]{1,0:T(8,128)(2,1)S(1)} %shard_map.104.refs_1_, ...), custom_call_target="tpu_custom_call" | custom-call | tf_op jit(solution)/shard_map/pallas_call | solution.py:34
  51.0 6.1 %shard_map.106 = (bf16[96,384]{1,0:T(8,128)(2,1)S(1)}, bf16[96,384]{1,0:T(8,128)(2,1)S(1)}, bf16[96,384]{1,0:T(8,128)(2,1)S(1)}, bf16[96,384]{1,0:T(8,128)(2,1)S(1)}) custom-call(f32[8,8]{1,0:T(8,128)S(1)} %convert_add_fusion.refs_0_, bf16[768,640]{1,0:T(8,128)(2,1)S(1)} %shard_map.104.refs_1_, bf16[192,768]{1,0:T(8,128)(2,1)S(1)} %collective-permute-done.9.refs_2_, ...), custom_call_target="tpu_custom_call" | custom-call | tf_op jit(solution)/shard_map/pallas_call | solution.py:34
  57.3 2.2 %collective-permute-start.22 = (bf16[96,384]{1,0:T(8,128)(2,1)S(1)}, bf16[96,384]{1,0:T(8,128)(2,1)S(1)}, u32[]{:S(2)}, u32[]{:S(2)}) collective-permute-start(bf16[96,384]{1,0:T(8,128)(2,1)S(1)} %get-tuple-element.35), channel_id=1, source_target_pairs={{0,4},{1,5},{2,6},{3,7},{4,0},{5,1},{6,2},{7,3},{8,12},{9,13},{10,... | collective-permute-start | bytes 221192 | tf_op jit(solution)/shard_map/ppermute | solution.py:350
  59.4 2.2 %collective-permute-start.23 = (bf16[96,384]{1,0:T(8,128)(2,1)S(1)}, bf16[96,384]{1,0:T(8,128)(2,1)S(1)}, u32[]{:S(2)}, u32[]{:S(2)}) collective-permute-start(bf16[96,384]{1,0:T(8,128)(2,1)S(1)} %get-tuple-element.36), channel_id=1, source_target_pairs={{0,6},{1,7},{2,4},{3,5},{4,2},{5,3},{6,0},{7,1},{8,14},{9,15},{10,... | collective-permute-start | bytes 221192 | tf_op jit(solution)/shard_map/ppermute | solution.py:350
  61.7 0.7 %collective-permute-done.21.refs_2_ = bf16[96,384]{1,0:T(8,128)(2,1)S(1)} collective-permute-done((bf16[96,384]{1,0:T(8,128)(2,1)S(1)}, bf16[96,384]{1,0:T(8,128)(2,1)S(1)}, u32[]{:S(2)}, u32[]{:S(2)}) %collective-permute-start.21) | collective-permute-done | bytes 73760 | tf_op jit(solution)/shard_map/ppermute | solution.py:350
  62.5 4.1 %collective-permute-done.22.refs_3_ = bf16[96,384]{1,0:T(8,128)(2,1)S(1)} collective-permute-done((bf16[96,384]{1,0:T(8,128)(2,1)S(1)}, bf16[96,384]{1,0:T(8,128)(2,1)S(1)}, u32[]{:S(2)}, u32[]{:S(2)}) %collective-permute-start.22) | collective-permute-done | bytes 73760 | tf_op jit(solution)/shard_map/ppermute | solution.py:350
  66.5 1.3 %shard_map.107 = bf16[192,768]{1,0:T(8,128)(2,1)} custom-call(bf16[768,768]{1,0:T(8,128)(2,1)S(1)} %shard_map.103.refs_0_, bf16[96,384]{1,0:T(8,128)(2,1)S(1)} %get-tuple-element.33.refs_1_, bf16[96,384]{1,0:T(8,128)(2,1)S(1)} %collective-permute-done.21.refs_2_, bf16[96,384]{1,0:T(8,128)(2,1)S(1)} %collective-permute-done.22.refs_3_, ...), custom_call_target="tpu_custom_call" | custom-call | tf_op jit(solution)/shard_map/pallas_call | solution.py:34
  (39 shorter events, 4.8 us)
Async XLA Ops:
  3.1 5.1 %collective-permute-start.10 = (bf16[192,768]{1,0:T(8,128)(2,1)}, bf16[192,768]{1,0:T(8,128)(2,1)S(1)}, u32[]{:S(2)}, u32[]{:S(2)}) collective-permute-start(bf16[192,768]{1,0:T(8,128)(2,1)} %get-tuple-element.27.refs_2_), channel_id=1, source_target_pairs={{0,1},{1,0},{2,3},{3,2},{4,5},{5,4},{6,7},{7,6},{8,9},{9,8},{10,11... | collective-permute-start | bytes 884744 | tf_op jit(solution)/shard_map/ppermute | solution.py:355
  3.7 20.7 %collective-permute-start.8 = (bf16[192,768]{1,0:T(8,128)(2,1)}, bf16[192,768]{1,0:T(8,128)(2,1)S(1)}, u32[]{:S(2)}, u32[]{:S(2)}) collective-permute-start(bf16[192,768]{1,0:T(8,128)(2,1)} %get-tuple-element.27.refs_2_), channel_id=1, source_target_pairs={{0,2},{2,4},{4,6},{3,1},{5,3},{7,5},{8,10},{10,12},{12,14},{11,9},... | collective-permute-start | bytes 884744 | tf_op jit(solution)/shard_map/ppermute | solution.py:384
  8.2 16.9 %collective-permute-start.11 = (bf16[192,768]{1,0:T(8,128)(2,1)S(1)}, bf16[192,768]{1,0:T(8,128)(2,1)S(1)}, u32[]{:S(2)}, u32[]{:S(2)}) collective-permute-start(bf16[192,768]{1,0:T(8,128)(2,1)S(1)} %collective-permute-done.10.refs_3_), channel_id=1, source_target_pairs={{0,2},{2,4},{4,6},{3,1},{5,3},{7,5},{8,10},{10,12},{12,14},{11,9},... | collective-permute-start | bytes 884744 | tf_op jit(solution)/shard_map/ppermute | solution.py:384
  11.7 7.1 %collective-permute-start = (bf16[24,1408]{1,0:T(8,128)(2,1)}, bf16[24,1408]{1,0:T(8,128)(2,1)S(1)}, u32[]{:S(2)}, u32[]{:S(2)}) collective-permute-start(bf16[24,1408]{1,0:T(8,128)(2,1)} %get-tuple-element.22), channel_id=1, source_target_pairs={{0,2},{1,3},{2,0},{3,1},{4,6},{5,7},{6,4},{7,5},{8,10},{9,11},{10,... | collective-permute-start | bytes 202760 | tf_op jit(solution)/shard_map/ppermute | solution.py:350
  13.3 7.5 %collective-permute-start.1 = (bf16[24,1408]{1,0:T(8,128)(2,1)}, bf16[24,1408]{1,0:T(8,128)(2,1)S(1)}, u32[]{:S(2)}, u32[]{:S(2)}) collective-permute-start(bf16[24,1408]{1,0:T(8,128)(2,1)} %get-tuple-element.23), channel_id=1, source_target_pairs={{0,4},{1,5},{2,6},{3,7},{4,0},{5,1},{6,2},{7,3},{8,12},{9,13},{10,... | collective-permute-start | bytes 202760 | tf_op jit(solution)/shard_map/ppermute | solution.py:350
  13.3 7.5 %collective-permute-start.2 = (bf16[24,1408]{1,0:T(8,128)(2,1)}, bf16[24,1408]{1,0:T(8,128)(2,1)S(1)}, u32[]{:S(2)}, u32[]{:S(2)}) collective-permute-start(bf16[24,1408]{1,0:T(8,128)(2,1)} %get-tuple-element.24), channel_id=1, source_target_pairs={{0,6},{1,7},{2,4},{3,5},{4,2},{5,3},{6,0},{7,1},{8,14},{9,15},{10,... | collective-permute-start | bytes 202760 | tf_op jit(solution)/shard_map/ppermute | solution.py:350
  20.9 7.3 %collective-permute-start.3 = (bf16[72,1408]{1,0:T(8,128)(2,1)S(1)}, bf16[72,1408]{1,0:T(8,128)(2,1)S(1)}, u32[]{:S(2)}, u32[]{:S(2)}) collective-permute-start(bf16[72,1408]{1,0:T(8,128)(2,1)S(1)} %shard_map.101.refs_0_), channel_id=1, source_target_pairs={{0,8},{1,9},{2,10},{3,11},{4,12},{5,13},{6,14},{7,15},{8,0},{9,1},... | collective-permute-start | bytes 608264 | tf_op jit(solution)/shard_map/ppermute | solution.py:356
  22.4 11.8 %collective-permute-start.4 = (bf16[72,1408]{1,0:T(8,128)(2,1)S(1)}, bf16[72,1408]{1,0:T(8,128)(2,1)S(1)}, u32[]{:S(2)}, u32[]{:S(2)}) collective-permute-start(bf16[72,1408]{1,0:T(8,128)(2,1)S(1)} %shard_map.101.refs_0_), channel_id=1, source_target_pairs={{0,16},{1,17},{2,18},{3,19},{4,20},{5,21},{6,22},{7,23},{8,24},{9,... | collective-permute-start | bytes 608264 | tf_op jit(solution)/shard_map/ppermute | solution.py:356
  23.9 10.3 %collective-permute-start.5 = (bf16[72,1408]{1,0:T(8,128)(2,1)S(1)}, bf16[72,1408]{1,0:T(8,128)(2,1)S(1)}, u32[]{:S(2)}, u32[]{:S(2)}) collective-permute-start(bf16[72,1408]{1,0:T(8,128)(2,1)S(1)} %shard_map.101.refs_0_), channel_id=1, source_target_pairs={{0,24},{1,25},{2,26},{3,27},{4,28},{5,29},{6,30},{7,31},{8,16},{9,... | collective-permute-start | bytes 608264 | tf_op jit(solution)/shard_map/ppermute | solution.py:356
  24.4 11.6 %collective-permute-start.9 = (bf16[192,768]{1,0:T(8,128)(2,1)S(1)}, bf16[192,768]{1,0:T(8,128)(2,1)S(1)}, u32[]{:S(2)}, u32[]{:S(2)}) collective-permute-start(bf16[192,768]{1,0:T(8,128)(2,1)S(1)} %collective-permute-done.8.refs_4_), channel_id=1, source_target_pairs={{2,4},{4,6},{3,1},{5,3},{10,12},{12,14},{11,9},{13,11},{18,20},{20... | collective-permute-start | bytes 884744 | tf_op jit(solution)/shard_map/ppermute | solution.py:384
  25.1 11.6 %collective-permute-start.12 = (bf16[192,768]{1,0:T(8,128)(2,1)S(1)}, bf16[192,768]{1,0:T(8,128)(2,1)S(1)}, u32[]{:S(2)}, u32[]{:S(2)}) collective-permute-start(bf16[192,768]{1,0:T(8,128)(2,1)S(1)} %collective-permute-done.11.refs_5_), channel_id=1, source_target_pairs={{2,4},{4,6},{3,1},{5,3},{10,12},{12,14},{11,9},{13,11},{18,20},{20... | collective-permute-start | bytes 884744 | tf_op jit(solution)/shard_map/ppermute | solution.py:384
  28.1 9.2 %collective-permute-start.19 = (bf16[192,768]{1,0:T(8,128)(2,1)S(1)}, bf16[192,768]{1,0:T(8,128)(2,1)S(1)}, u32[]{:S(2)}, u32[]{:S(2)}) collective-permute-start(bf16[192,768]{1,0:T(8,128)(2,1)S(1)} %collective-permute-done.8.refs_4_), channel_id=1, source_target_pairs={{0,1},{1,0},{2,3},{3,2},{4,5},{5,4},{6,7},{7,6},{8,9},{9,8},{10,11... | collective-permute-start | bytes 884744 | tf_op jit(solution)/shard_map/ppermute | solution.py:355
  35.4 3.5 %collective-permute-start.7 = (bf16[384,640]{1,0:T(8,128)(2,1)S(1)}, bf16[384,640]{1,0:T(8,128)(2,1)S(1)}, u32[]{:S(2)}, u32[]{:S(2)}) collective-permute-start(bf16[384,640]{1,0:T(8,128)(2,1)S(1)} %get-tuple-element.26.mine_ref), channel_id=1, source_target_pairs={{0,1},{1,0},{2,3},{3,2},{4,5},{5,4},{6,7},{7,6},{8,9},{9,8},{10,11... | collective-permute-start | bytes 1474568 | tf_op jit(solution)/shard_map/ppermute | solution.py:355
  35.7 3.3 %collective-permute-start.20 = (bf16[192,768]{1,0:T(8,128)(2,1)S(1)}, bf16[192,768]{1,0:T(8,128)(2,1)S(1)}, u32[]{:S(2)}, u32[]{:S(2)}) collective-permute-start(bf16[192,768]{1,0:T(8,128)(2,1)S(1)} %collective-permute-done.11.refs_5_), channel_id=1, source_target_pairs={{0,1},{1,0},{2,3},{3,2},{4,5},{5,4},{6,7},{7,6},{8,9},{9,8},{10,11... | collective-permute-start | bytes 884744 | tf_op jit(solution)/shard_map/ppermute | solution.py:355
  36.0 3.4 %collective-permute-start.15 = (bf16[192,768]{1,0:T(8,128)(2,1)S(1)}, bf16[192,768]{1,0:T(8,128)(2,1)S(1)}, u32[]{:S(2)}, u32[]{:S(2)}) collective-permute-start(bf16[192,768]{1,0:T(8,128)(2,1)S(1)} %collective-permute-done.9.refs_2_), channel_id=1, source_target_pairs={{4,6},{3,1},{12,14},{11,9},{20,22},{19,17},{28,30},{27,25}} | collective-permute-start | bytes 884744 | tf_op jit(solution)/shard_map/ppermute | solution.py:384
  36.7 7.0 %collective-permute-start.16 = (bf16[192,768]{1,0:T(8,128)(2,1)S(1)}, bf16[192,768]{1,0:T(8,128)(2,1)S(1)}, u32[]{:S(2)}, u32[]{:S(2)}) collective-permute-start(bf16[192,768]{1,0:T(8,128)(2,1)S(1)} %collective-permute-done.12.refs_3_), channel_id=1, source_target_pairs={{4,6},{3,1},{12,14},{11,9},{20,22},{19,17},{28,30},{27,25}} | collective-permute-start | bytes 884744 | tf_op jit(solution)/shard_map/ppermute | solution.py:384
  37.4 24.3 %collective-permute-start.6 = (bf16[384,768]{1,0:T(8,128)(2,1)S(1)}, bf16[384,768]{1,0:T(8,128)(2,1)S(1)}, u32[]{:S(2)}, u32[]{:S(2)}) collective-permute-start(bf16[384,768]{1,0:T(8,128)(2,1)S(1)} %get-tuple-element.25.mine_ref), channel_id=1, source_target_pairs={{0,1},{1,0},{2,3},{3,2},{4,5},{5,4},{6,7},{7,6},{8,9},{9,8},{10,11... | collective-permute-start | bytes 1769480 | tf_op jit(solution)/shard_map/ppermute | solution.py:355
  38.9 12.1 %collective-permute-start.13 = (bf16[192,768]{1,0:T(8,128)(2,1)S(1)}, bf16[192,768]{1,0:T(8,128)(2,1)S(1)}, u32[]{:S(2)}, u32[]{:S(2)}) collective-permute-start(bf16[192,768]{1,0:T(8,128)(2,1)S(1)} %collective-permute-done.9.refs_2_), channel_id=1, source_target_pairs={{0,1},{1,0},{2,3},{3,2},{4,5},{5,4},{6,7},{7,6},{8,9},{9,8},{10,11... | collective-permute-start | bytes 884744 | tf_op jit(solution)/shard_map/ppermute | solution.py:355
  39.0 12.0 %collective-permute-start.14 = (bf16[192,768]{1,0:T(8,128)(2,1)S(1)}, bf16[192,768]{1,0:T(8,128)(2,1)S(1)}, u32[]{:S(2)}, u32[]{:S(2)}) collective-permute-start(bf16[192,768]{1,0:T(8,128)(2,1)S(1)} %collective-permute-done.12.refs_3_), channel_id=1, source_target_pairs={{0,1},{1,0},{2,3},{3,2},{4,5},{5,4},{6,7},{7,6},{8,9},{9,8},{10,11... | collective-permute-start | bytes 884744 | tf_op jit(solution)/shard_map/ppermute | solution.py:355
  39.4 11.6 %collective-permute-start.17 = (bf16[192,768]{1,0:T(8,128)(2,1)S(1)}, bf16[192,768]{1,0:T(8,128)(2,1)S(1)}, u32[]{:S(2)}, u32[]{:S(2)}) collective-permute-start(bf16[192,768]{1,0:T(8,128)(2,1)S(1)} %collective-permute-done.15.refs_6_), channel_id=1, source_target_pairs={{0,1},{1,0},{2,3},{3,2},{4,5},{5,4},{6,7},{7,6},{8,9},{9,8},{10,11... | collective-permute-start | bytes 884744 | tf_op jit(solution)/shard_map/ppermute | solution.py:355
  43.7 7.4 %collective-permute-start.18 = (bf16[192,768]{1,0:T(8,128)(2,1)S(1)}, bf16[192,768]{1,0:T(8,128)(2,1)S(1)}, u32[]{:S(2)}, u32[]{:S(2)}) collective-permute-start(bf16[192,768]{1,0:T(8,128)(2,1)S(1)} %collective-permute-done.16.refs_7_), channel_id=1, source_target_pairs={{0,1},{1,0},{2,3},{3,2},{4,5},{5,4},{6,7},{7,6},{8,9},{9,8},{10,11... | collective-permute-start | bytes 884744 | tf_op jit(solution)/shard_map/ppermute | solution.py:355
  57.2 5.3 %collective-permute-start.21 = (bf16[96,384]{1,0:T(8,128)(2,1)S(1)}, bf16[96,384]{1,0:T(8,128)(2,1)S(1)}, u32[]{:S(2)}, u32[]{:S(2)}) collective-permute-start(bf16[96,384]{1,0:T(8,128)(2,1)S(1)} %get-tuple-element.34), channel_id=1, source_target_pairs={{0,2},{1,3},{2,0},{3,1},{4,6},{5,7},{6,4},{7,5},{8,10},{9,11},{10,... | collective-permute-start | bytes 221192 | tf_op jit(solution)/shard_map/ppermute | solution.py:350
  57.3 9.3 %collective-permute-start.22 = (bf16[96,384]{1,0:T(8,128)(2,1)S(1)}, bf16[96,384]{1,0:T(8,128)(2,1)S(1)}, u32[]{:S(2)}, u32[]{:S(2)}) collective-permute-start(bf16[96,384]{1,0:T(8,128)(2,1)S(1)} %get-tuple-element.35), channel_id=1, source_target_pairs={{0,4},{1,5},{2,6},{3,7},{4,0},{5,1},{6,2},{7,3},{8,12},{9,13},{10,... | collective-permute-start | bytes 221192 | tf_op jit(solution)/shard_map/ppermute | solution.py:350
  59.4 7.1 %collective-permute-start.23 = (bf16[96,384]{1,0:T(8,128)(2,1)S(1)}, bf16[96,384]{1,0:T(8,128)(2,1)S(1)}, u32[]{:S(2)}, u32[]{:S(2)}) collective-permute-start(bf16[96,384]{1,0:T(8,128)(2,1)S(1)} %get-tuple-element.36), channel_id=1, source_target_pairs={{0,6},{1,7},{2,4},{3,5},{4,2},{5,3},{6,0},{7,1},{8,14},{9,15},{10,... | collective-permute-start | bytes 221192 | tf_op jit(solution)/shard_map/ppermute | solution.py:350
  (3 other events, 46.8 us)
